TPU v7x, 128 devices: a whole 4x4x4 slice. The times are simulated.
128 devices in a mesh: row: 16 (over y, x), col: 8 (over z, core).
Axes of the slice: x: 4, y: 4, z: 4, core: 2. Of those that a mesh axis runs over, the one named last changes fastest.
Arguments:
- front: float32 [8192, 8192], P('row', 'col'), may hold values from -1 to 4, as said below
- mass_diag: float32 [8192], replicated, may hold values from 0.5 to 1
- shift_bounds: int32 [2], replicated, may hold values from 0 to 255
- vectors: float32 [64, 262144], P(None, ('row', 'col')), may hold values from -12 to 12
- basis: float32 [128, 262144], P(None, ('row', 'col')), may hold values from -6 to 6
- element_dofs: int32 [24, 65536], P(None, ('row', 'col')), may hold values from 0 to 2303
- face_dofs: int32 [256, 128], P(('row', 'col')), may hold values from 0 to 2047
- mass_blocks: float32 [24, 24, 65536], P(None, None, ('row', 'col')), may hold values from -37 to 37
Outputs:
- factor: float32 [8192, 8192], P('row', 'col')
- new_block: float32 [64, 262144], P(None, ('row', 'col'))
- projections: float32 [128, 64], replicated
- cholesky_factor: float32 [64, 64], replicated
Inputs may be any that keep to these rules, and one draw needn't show every extreme that they name: Symmetric; every leading principal block of the shifted front is positive definite. `element_dofs`: an entry below 2048 names one of the subdomain's own degrees of freedom; 2048 + j names the j-th of the 256 received ones.
All inputs are finite; a program needn't handle non-finite values.
Results may differ from a plain program's by a relative error of at most 0.0001.
Values sent between devices are 32-bit elements; how exact they have to be, the bound alone decides.
A program may use at most 128 MiB of HBM per device.

v0:
```python
import jax
import jax.numpy as jnp
from jax import lax
from jax.sharding import PartitionSpec as P

PB = 512
NPAN = 2


PRECISE = lax.Precision.HIGHEST


def from_root(value, axis, source):
    kept = jnp.where(lax.axis_index(axis) == source, value, 0).astype(value.dtype)
    return lax.psum(kept, axis)


def padded(cells, sides, width):
    for axis, dim in sides:
        count = lax.axis_size(axis)
        ends = count - 1
        head = lax.slice_in_dim(cells, 0, width, axis=dim)
        tail = lax.slice_in_dim(cells, cells.shape[dim] - width, cells.shape[dim], axis=dim)
        cells = jnp.concatenate(
            [
                lax.ppermute(tail, axis, [(i, (i + 1) % count) for i in range(ends)]),
                cells,
                lax.ppermute(head, axis, [((i + 1) % count, i) for i in range(ends)]),
            ],
            axis=dim,
        )
    return cells


def product(left, right):
    return jnp.dot(left, right, precision=PRECISE, preferred_element_type=jnp.float32)


def inner_rows(left, right):
    return lax.dot_general(
        left, right, (((1,), (1,)), ((), ())), precision=PRECISE, preferred_element_type=jnp.float32
    )


def invert_block(block):
    factor = jnp.linalg.cholesky(block)
    identity = jnp.eye(block.shape[0], dtype=block.dtype)
    return jax.scipy.linalg.cho_solve((factor, True), identity)


def shards(front, mass_diag, shift_bounds, vectors, basis, element_dofs, face_dofs, mass_blocks):
    row_count, col_count = front.shape
    row_index = lax.axis_index("row")
    col_index = lax.axis_index("col")
    global_rows = row_index * row_count + jnp.arange(row_count, dtype=jnp.int32)
    global_cols = col_index * col_count + jnp.arange(col_count, dtype=jnp.int32)
    shift_value = (shift_bounds[0] + shift_bounds[1]).astype(jnp.float32) / 510.0
    local_mass = lax.dynamic_slice_in_dim(mass_diag, col_index * col_count, col_count)
    on_diagonal = global_rows[:, None] == global_cols[None, :]
    matrix = front - jnp.where(on_diagonal, shift_value * local_mass[None, :], 0.0)
    blank_rows = jnp.zeros((PB, col_count), jnp.float32)
    for panel_index in range(NPAN):
        begin_at = panel_index * PB
        end_at = begin_at + PB
        col_root = begin_at // col_count
        col_offset = begin_at % col_count
        row_root = begin_at // row_count
        column_panel = from_root(matrix[:, col_offset : col_offset + PB], "col", col_root)
        diag_block = column_panel
        on_root = row_index == row_root
        row_panel, diag_block = (
            from_root(matrix, "row", row_root),
            from_root(diag_block, "row", row_root),
        )
        inverse = invert_block(diag_block)
        left_factor = product(column_panel, inverse)
        update = product(left_factor, row_panel)
        right_factor = lax.cond(on_root, lambda: product(inverse, row_panel), lambda: blank_rows)
        trail_rows = global_rows >= end_at
        trail_cols = global_cols >= end_at
        panel_rows = (global_rows >= begin_at) & (global_rows < end_at)
        panel_cols = (global_cols >= begin_at) & (global_cols < end_at)
        left_wide = jnp.pad(left_factor, ((0, 0), (col_offset, col_count - col_offset - PB)))
        matrix = jnp.where(trail_rows[:, None] & trail_cols[None, :], matrix - update, matrix)
        matrix = jnp.where(trail_rows[:, None] & panel_cols[None, :], left_wide, matrix)
        matrix = jnp.where(panel_rows[:, None] & trail_cols[None, :], right_factor, matrix)
    owned = vectors.shape[1]
    outgoing = jnp.stack([vectors[:, face_dofs[0]], vectors[:, face_dofs[1]]])
    received = padded(outgoing, ((("row", "col"), 0),), 1)
    extended = jnp.concatenate([vectors, received[0], received[3]], axis=1)
    gathered = extended[:, element_dofs]
    contrib = jnp.einsum("abe,vbe->vae", mass_blocks, gathered, precision=PRECISE)
    applied = jnp.zeros_like(extended).at[:, element_dofs].add(contrib)[:, :owned]
    total_dofs = owned * lax.axis_size("row") * lax.axis_size("col")
    projections = lax.psum(inner_rows(basis, applied), ("row", "col")) / total_dofs
    corrected = applied - product(projections.T, basis)
    gram_matrix = lax.psum(inner_rows(corrected, corrected), ("row", "col")) / total_dofs
    cholesky_factor = jnp.linalg.cholesky(gram_matrix)
    new_block = jax.scipy.linalg.solve_triangular(cholesky_factor, corrected, lower=True)
    return (matrix, new_block, projections, cholesky_factor)


def solution(mesh):
    placed = (
        P("row", "col"),
        P(),
        P(),
        P(None, ("row", "col")),
        P(None, ("row", "col")),
        P(None, ("row", "col")),
        P(("row", "col"), None),
        P(None, None, ("row", "col")),
    )
    return jax.shard_map(
        shards,
        mesh=mesh,
        in_specs=placed,
        out_specs=(P("row", "col"), P(None, ("row", "col")), P(), P()),
        check_vma=False,
    )
```

profile of v0, /device:TPU:42, one launch (start us, length us, event | category | flops | bytes accessed | tf_op | source)
XLA Modules:
  0.0 895.3 jit_solution(4057479114357901695)
XLA Ops:
  17.9 62.5 %all-reduce.10.cloned.1.call-done = f32[512,512]{0,1:T(8,128)} async-done(((f32[512,512]{0,1:T(8,128)}), f32[512,512]{0,1:T(8,128)}) %all-reduce.10.cloned.1.call-update) | async-done | bytes 1048592 | tf_op jit(solution)/shard_map/psum | solution.py:15
  101.3 78.3 %all-reduce.16.cloned.1.call-done = (f32[512,512]{0,1:T(8,128)}, f32[512,1024]{0,1:T(8,128)}) async-done(((f32[512,512]{0,1:T(8,128)}, f32[512,1024]{0,1:T(8,128)}), (f32[512,512]{0,1:T(8,128)}, f32[512,1024]{0,1:T(8,128)})) %all-reduce.16.cloned.1.call-update) | async-done | bytes 3145744 | tf_op jit(solution)/shard_map/psum | solution.py:15
  184.9 11.7 %cholesky.321 = f32[128,128]{1,0:T(8,128)S(1)} custom-call(f32[128,128]{1,0:T(8,128)S(1)} %cholesky.461), custom_call_target="Cholesky" | custom-call | tf_op jit(solution)/shard_map/jit(cholesky)/cholesky | solution.py:46
  196.7 9.8 %custom-call.37 = f32[1,128,128]{1,2,0:T(8,128)S(1)} custom-call(f32[1,128,128]{2,1,0:T(8,128)S(1)} %get-tuple-element.105), custom_call_target="InvertDiagBlocksLowerTriangular" | custom-call | tf_op jit(solution)/shard_map/jit(cholesky)/cholesky | solution.py:46
  211.4 12.5 %cholesky.340 = f32[128,128]{1,0:T(8,128)S(1)} custom-call(f32[128,128]{1,0:T(8,128)} %cholesky.465), custom_call_target="Cholesky" | custom-call | tf_op jit(solution)/shard_map/jit(cholesky)/cholesky | solution.py:46
  224.6 10.9 %custom-call.38 = f32[1,128,128]{1,2,0:T(8,128)S(1)} custom-call(f32[1,128,128]{2,1,0:T(8,128)} %get-tuple-element.102), custom_call_target="InvertDiagBlocksLowerTriangular" | custom-call | tf_op jit(solution)/shard_map/jit(cholesky)/cholesky | solution.py:46
  237.9 11.7 %cholesky.361 = f32[128,128]{1,0:T(8,128)S(1)} custom-call(f32[128,128]{1,0:T(8,128)S(1)} %cholesky.470), custom_call_target="Cholesky" | custom-call | tf_op jit(solution)/shard_map/jit(cholesky)/cholesky | solution.py:46
  263.0 11.7 %cholesky.378 = f32[128,128]{1,0:T(8,128)S(1)} custom-call(f32[128,128]{1,0:T(8,128)S(1)} %convolution_subtract_fusion.18), custom_call_target="Cholesky" | custom-call | tf_op jit(solution)/shard_map/jit(cholesky)/cholesky | solution.py:46
  276.0 13.1 %compare_reduce_fusion.6 = (pred[]{:T(512)}, pred[]{:T(512)}) fusion(f32[128]{0:T(128)S(1)} %get-tuple-element.101, f32[128]{0:T(128)S(1)} %get-tuple-element.104), kind=kLoop, calls=%fused_computation.216 | loop fusion | flops 510 | bytes 1026 | tf_op jit(solution)/shard_map/jit(cholesky)/cholesky | solution.py:46
  294.7 11.2 %while.4 = (s32[]{:T(128)}, f32[512,512]{1,0:T(8,128)}, s32[4,2]{0,1:T(2,128)S(1)}, f32[4,128,128]{2,1,0:T(8,128)S(1)}, s32[]{:T(128)}) while((s32[]{:T(128)}, f32[512,512]{1,0:T(8,128)}, s32[4,2]{0,1:T(2,128)S(1)}, f32[4,128,128]{2,1,0:T(8,128)S(1)}, s32[]{:T(128)}) %tuple.91), condition=%wide.while_cond, body=%wide.while_body.sunk | while | flops 2 | bytes 131181 | solution.py:48
  306.7 40.1 %custom-call.40 = f32[4,128,128]{1,2,0:T(8,128)S(1)} custom-call(f32[4,128,128]{2,1,0:T(8,128)} %copy-done.16), custom_call_target="InvertDiagBlocksLowerTriangular" | custom-call | tf_op jit(solution)/shard_map/jit(_cho_solve)/triangular_solve | solution.py:48
  375.3 63.7 %all-reduce.12.cloned.1.call-done = f32[512,512]{0,1:T(8,128)} async-done(((f32[512,512]{0,1:T(8,128)}), f32[512,512]{0,1:T(8,128)}) %all-reduce.12.cloned.1.call-update) | async-done | bytes 1048592 | tf_op jit(solution)/shard_map/psum | solution.py:15
  442.2 41.0 %gather_fusion.2 = f32[12288,64]{1,0:T(8,128)} fusion(f32[64,2304]{0,1:T(8,128)S(1)} %pad_maximum_fusion, s32[12288]{0:T(1024)S(1)} %broadcast_clamp_fusion), kind=kCustom, calls=%fused_computation.2 | custom fusion | bytes 6340608 | tf_op jit(solution)/shard_map/gather | solution.py:91
  483.2 17.6 %fusion.3 = f32[24,512,64]{2,0,1:T(8,128)S(1)} fusion(f32[24,24,512]{1,0,2:T(8,128)} %copy.47, f32[24,512,64]{2,1,0:T(8,128)} %bitcast.171), kind=kOutput, calls=%fused_computation.13 | convolution fusion | flops 226492416 | bytes 7471104 | tf_op jit(solution)/shard_map/abe,vbe->vae/dot_general | solution.py:92
  504.7 66.4 %scatter_custom_fusion = f32[64,2304]{0,1:T(8,128)S(1)} fusion(s32[12288]{0:T(1024)S(1)} %bitcast.174, f32[12288,64]{1,0:T(8,128)} %bitcast.172, f32[]{:T(128)} %constant.193.clone.1), kind=kCustom, calls=%fused_computation.79 | custom fusion | flops 786432 | bytes 590336 | tf_op jit(solution)/shard_map/scatter-add | solution.py:93
  574.1 64.4 %psum.62 = f32[128,64]{0,1:T(8,128)S(1)} all-reduce(f32[128,64]{0,1:T(8,128)S(1)} %convolution_bitcast_fusion), channel_id=1, replica_groups=mesh['row'=16,'col'=8] {'row','col'}, use_global_device_ids=true, to_apply=%region_19.22 | all-reduce | flops 8192 | bytes 65536 | tf_op jit(solution)/shard_map/psum | solution.py:95
  639.8 63.3 %psum.63 = f32[64,64]{0,1:T(8,128)S(1)} all-reduce(f32[64,64]{0,1:T(8,128)S(1)} %fusion.143), channel_id=1, replica_groups=mesh['row'=16,'col'=8] {'row','col'}, use_global_device_ids=true, to_apply=%region_20.23 | all-reduce | flops 4096 | bytes 32768 | tf_op jit(solution)/shard_map/psum | solution.py:97
  720.2 11.7 %cholesky.393 = f32[128,128]{1,0:T(8,128)S(1)} custom-call(f32[128,128]{1,0:T(8,128)S(1)} %cholesky.474), custom_call_target="Cholesky" | custom-call | tf_op jit(solution)/shard_map/jit(cholesky)/cholesky | solution.py:46
  732.1 9.8 %custom-call.41 = f32[1,128,128]{1,2,0:T(8,128)S(1)} custom-call(f32[1,128,128]{2,1,0:T(8,128)S(1)} %get-tuple-element.95), custom_call_target="InvertDiagBlocksLowerTriangular" | custom-call | tf_op jit(solution)/shard_map/jit(cholesky)/cholesky | solution.py:46
  744.5 12.1 %cholesky.412 = f32[128,128]{1,0:T(8,128)S(1)} custom-call(f32[128,128]{1,0:T(8,128)S(1)} %cholesky.478), custom_call_target="Cholesky" | custom-call | tf_op jit(solution)/shard_map/jit(cholesky)/cholesky | solution.py:46
  769.3 11.7 %cholesky.433 = f32[128,128]{1,0:T(8,128)S(1)} custom-call(f32[128,128]{1,0:T(8,128)S(1)} %cholesky.483), custom_call_target="Cholesky" | custom-call | tf_op jit(solution)/shard_map/jit(cholesky)/cholesky | solution.py:46
  792.9 11.9 %cholesky.450 = f32[128,128]{1,0:T(8,128)S(1)} custom-call(f32[128,128]{1,0:T(8,128)S(1)} %convolution_subtract_fusion.17), custom_call_target="Cholesky" | custom-call | tf_op jit(solution)/shard_map/jit(cholesky)/cholesky | solution.py:46
  809.7 13.8 %while.5 = (s32[]{:T(128)}, f32[512,512]{1,0:T(8,128)}, s32[4,2]{0,1:T(2,128)S(1)}, f32[4,128,128]{2,1,0:T(8,128)}, s32[]{:T(128)}) while((s32[]{:T(128)}, f32[512,512]{1,0:T(8,128)}, s32[4,2]{0,1:T(2,128)S(1)}, f32[4,128,128]{2,1,0:T(8,128)}, s32[]{:T(128)}) %tuple.111), condition=%wide.while_cond.clone, body=%wide.while_body.clone.sunk | while | flops 2 | bytes 132705 | solution.py:48
  823.5 40.2 %custom-call.44 = f32[4,128,128]{1,2,0:T(8,128)S(1)} custom-call(f32[4,128,128]{2,1,0:T(8,128)} %get-tuple-element.39), custom_call_target="InvertDiagBlocksLowerTriangular" | custom-call | tf_op jit(solution)/shard_map/jit(_cho_solve)/triangular_solve | solution.py:48
  (206 shorter events, 199.6 us)
Async XLA Ops:
  7.2 565.1 %copy-start = (f32[128,2048]{1,0:T(8,128)S(1)}, f32[128,2048]{1,0:T(8,128)}, u32[]{:S(2)}) copy-start(f32[128,2048]{1,0:T(8,128)} %param.19) | copy-start | bytes 3145732
  7.2 73.2 %all-reduce.10.cloned.1.call-start = ((), (), s32[]{:S(2)}) async-start(), calls=%async_computation | async-start | bytes 2097152 | tf_op jit(solution)/shard_map/psum | solution.py:15
  17.9 161.8 %all-reduce.16.cloned.1.call-start = ((), (), s32[]{:S(2)}) async-start(), calls=%async_computation.3 | async-start | bytes 6291456 | tf_op jit(solution)/shard_map/psum | solution.py:15
  81.5 2.5 copy-start.19
  81.5 13.0 %copy-start.18 = (s32[24,512]{1,0:T(8,128)S(1)}, s32[24,512]{1,0:T(8,128)}, u32[]{:S(2)}) copy-start(s32[24,512]{1,0:T(8,128)} %param.20) | copy-start | bytes 147460
  81.5 357.5 %all-reduce.12.cloned.1.call-start = ((), (), s32[]{:S(2)}) async-start(), calls=%async_computation.1 | async-start | bytes 2097152 | tf_op jit(solution)/shard_map/psum | solution.py:15
  86.5 353.6 %collective-permute-start = (f32[1,64,128]{1,2,0:T(8,128)}, f32[1,64,128]{1,2,0:T(8,128)S(1)}, u32[]{:S(2)}, u32[]{:S(2)}) collective-permute-start(f32[1,64,128]{1,2,0:T(8,128)} %bitcast.26), channel_id=1, source_target_pairs={{0,1},{1,2},{2,3},{3,4},{4,5},{5,6},{6,7},{7,8},{8,9},{9,10},{10,1... | collective-permute-start | bytes 98312 | tf_op jit(solution)/shard_map/ppermute | solution.py:26
  90.9 349.2 %collective-permute-start.1 = (f32[1,64,128]{1,2,0:T(8,128)}, f32[1,64,128]{1,2,0:T(8,128)}, u32[]{:S(2)}, u32[]{:S(2)}) collective-permute-start(f32[1,64,128]{1,2,0:T(8,128)} %bitcast.31), channel_id=1, source_target_pairs={{1,0},{2,1},{3,2},{4,3},{5,4},{6,5},{7,6},{8,7},{9,8},{10,9},{11,1... | collective-permute-start | bytes 98312 | tf_op jit(solution)/shard_map/ppermute | solution.py:28
  183.9 1.0 copy-start.14
  346.8 3.3 copy-start.4
  346.8 5.1 copy-start.9
  355.0 2.1 copy-start.11
  362.8 1.3 copy-start.6
  372.4 1.4 copy-start.1
  374.8 342.5 %all-reduce.14.cloned.1.call-start = ((), (), s32[]{:S(2)}) async-start(), calls=%async_computation.2 | async-start | bytes 6291456 | tf_op jit(solution)/shard_map/psum | solution.py:15
  440.1 1.2 copy-start.7
  572.3 66.2 %copy-start.15 = (f32[64,2048]{1,0:T(8,128)S(1)}, f32[64,2048]{1,0:T(8,128)}, u32[]{:S(2)}) copy-start(f32[64,2048]{1,0:T(8,128)} %copy.65) | copy-start | bytes 1572868
  638.5 78.8 %copy-start.17 = (f32[128,64]{0,1:T(8,128)}, f32[128,64]{0,1:T(8,128)S(1)}, u32[]{:S(2)}) copy-start(f32[128,64]{0,1:T(8,128)S(1)} %broadcast_multiply_fusion.1) | copy-start | bytes 98308
  717.4 1.7 copy-start.12
  769.3 94.5 %copy-start.5 = (f32[512,512]{1,0:T(8,128)S(1)}, f32[512,512]{1,0:T(8,128)}, u32[]{:S(2)}) copy-start(f32[512,512]{1,0:T(8,128)} %fusion.12) | copy-start | bytes 3145732
  823.5 42.3 %copy-start.8 = (f32[512,512]{1,0:T(8,128)S(1)}, f32[512,512]{1,0:T(8,128)}, u32[]{:S(2)}) copy-start(f32[512,512]{1,0:T(8,128)} %get-tuple-element.238) | copy-start | bytes 3145732
  869.8 2.1 copy-start.10
  873.8 1.3 copy-start.3
  875.1 2.3 copy-start.2
  (2 other events, 1.7 us)
Sparse Core Ops, SparseCore 0:
  18.0 62.3 all-reduce.9
  84.4 95.1 all-reduce.15
  375.0 63.9 all-reduce.11
  442.8 95.1 all-reduce.13
where the time goes:
time: 909 us; the launch traced here: 895 us
  other arithmetic  352 us (39%)
  waiting for transfers between devices  205 us (23%)
  blocking collectives  128 us (14%)
  local copies, waits for them, and re-layouts  111 us (12%)
  matrix products  72.6 us (8%)
  between operations  21.1 us (2%)
    psum x4, waiting for transfers between devices, from_root(): return lax.psum(kept, axis)  204 us
    another operation x29, other arithmetic, invert_block(): factor = jnp.linalg.cholesky(block)  174 us
    another operation x7, other arithmetic, invert_block(): return jax.scipy.linalg.cho_solve((factor, True), identity)  86.4 us
    scatter-add x1, other arithmetic, shards(): jnp.zeros_like(extended).at[:, element_dofs].add(contrib)[:, :owned]  66.4 us
    psum x1, blocking collectives, shards(): lax.psum(inner_rows(basis, applied), ('row', 'col')) / total_dofs  64.4 us
    psum x1, blocking collectives, shards(): lax.psum(inner_rows(corrected, corrected), ('row', 'col')) / total_dofs  63.3 us
    gather x1, local copies, waits for them, and re-layouts, shards(): gathered = extended[:, element_dofs]  41 us
    another operation x27, local copies, waits for them, and re-layouts, invert_block(): return jax.scipy.linalg.cho_solve((factor, True), identity)  26.3 us
  transfers between devices with their start and end apart: 6, of which 3 were waited for; matrix products, arithmetic and copies ran while one was open for 39% of the time, Pallas kernels for 0%

commit v1 on v0

v1 whole, which is shorter than its diff:
```python
import functools

import jax
import jax.numpy as jnp
from jax import lax
from jax.experimental import pallas as pl
from jax.experimental.pallas import tpu as pltpu
from jax.sharding import PartitionSpec as P

MESH = pl.DeviceIdType.MESH
HI = lax.Precision.HIGHEST
F32 = jnp.float32
BF16 = jnp.bfloat16
PB = 512
TOTAL = 262144.0
VM = pl.BlockSpec(memory_space=pltpu.VMEM)
ANY = pl.BlockSpec(memory_space=pl.ANY)
NT = (((1,), (1,)), ((), ()))
NN = (((1,), (0,)), ((), ()))
TN = (((0,), (0,)), ((), ()))


def dot(a, b, dims=NN):
    return lax.dot_general(a, b, dims, precision=HI, preferred_element_type=F32)


def split(a):
    high = a.astype(BF16)
    return high, (a - high.astype(F32)).astype(BF16)


def dot3(a, b, dims=NN):
    (ah, al), (bh, bl) = a, b

    def one(l, r):
        return lax.dot_general(l, r, dims, preferred_element_type=F32)

    return one(ah, bh) + (one(ah, bl) + one(al, bh))


def place():
    row, col = lax.axis_index("row"), lax.axis_index("col")
    return row % 4, row // 4, col // 2, col % 2


def device(x, y, z, k):
    return ((y % 4) * 4 + (x % 4), (z % 4) * 2 + k)


def enter(peers):
    barrier = pltpu.get_barrier_semaphore()
    for peer in peers:
        pl.semaphore_signal(barrier, inc=1, device_id=peer, device_id_type=MESH)
    return barrier


def remote(src, dst, send, recv, peer):
    return pltpu.make_async_remote_copy(
        src_ref=src, dst_ref=dst, send_sem=send, recv_sem=recv, device_id=peer, device_id_type=MESH
    )


def pick(ext_ref, index, chunks):
    low = jnp.broadcast_to(index & 127, (64, 128))
    high = jnp.broadcast_to(index >> 7, (64, 128))
    found = jnp.take_along_axis(ext_ref[:, 0:128], low, axis=1)
    for c in range(1, chunks):
        found = jnp.where(high == c, jnp.take_along_axis(ext_ref[:, 128 * c : 128 * c + 128], low, axis=1), found)
    return found


def travel_kernel(
    front, vectors, dofs, faces, mass,
    xr, rp, pv, applied,
    ext, fs, got, wide, hot,
    rp_in, pv_in, xr_in, rpx, rpy, pvz, pvc, xrz, xrc, face_out, face_in,
):
    x, y, z, k = place()
    me = lax.axis_index("row") * 8 + lax.axis_index("col")
    before, after = (me + 127) % 128, (me + 1) % 128
    peers = [
        device(x + 1, y, z, k), device(x + 3, y, z, k), device(x, y + 1, z, k), device(x, y + 3, z, k),
        device(x, y, z + 1, k), device(x, y, z + 3, k), device(x, y, z, 1 - k),
        (before // 8, before % 8), (after // 8, after % 8),
    ]
    barrier = enter(peers)

    def rows(ref, m):
        return ref.at[pl.ds(pl.multiple_of(m * 64, 64), 64), :]

    def half(ref, m):
        return ref.at[pl.ds(pl.multiple_of(m * 64, 64), 64), pl.ds(512, 512)]

    for source in range(2):
        @pl.when((x == source) & (y == 0))
        def _():
            for m in range(8):
                pltpu.make_async_copy(rows(front, m), rows(rp, m + 8 * source), rp_in.at[m + 8 * source]).start()

    @pl.when((z == 0) & (k == 0))
    def _():
        for m in range(8):
            pltpu.make_async_copy(rows(front, m), rows(xr, m), xr_in.at[m]).start()

    ext[:, 0:2048] = vectors[...]
    fs[0] = pick(ext, faces[0], 16)
    fs[1] = pick(ext, faces[1], 16)

    @pl.when(me == 0)
    def _():
        ext[:, 2048:2176] = jnp.zeros((64, 128), F32)

    @pl.when(me == 127)
    def _():
        ext[:, 2176:2304] = jnp.zeros((64, 128), F32)

    pl.semaphore_wait(barrier, len(peers))

    to_before = remote(fs.at[0], ext.at[:, pl.ds(2176, 128)], face_out.at[0], face_in.at[0], (before // 8, before % 8))
    to_after = remote(fs.at[1], ext.at[:, pl.ds(2048, 128)], face_out.at[1], face_in.at[1], (after // 8, after % 8))

    @pl.when(me > 0)
    def _():
        to_before.start()

    @pl.when(me < 127)
    def _():
        to_after.start()

    def rp_hop(m):
        d = 1 - 2 * (m % 2)
        hx = ((x - m // 8) * d + 8) % 4
        hy = (y * d + 8) % 4
        c = rows(rp, m)
        along_x = remote(c, c, rpx.at[m], rp_in.at[m], device(x + d + 4, y, z, k))
        along_y = remote(c, c, rpy.at[m], rp_in.at[m], device(x, y + d + 4, z, k))
        return along_x, (y == 0) & (hx < 3), along_y, hy < 3

    def rp_event(m):
        ax, px, ay, py = rp_hop(m)
        ax.wait_recv()

        @pl.when(px)
        def _():
            ax.start()

        @pl.when(py)
        def _():
            ay.start()

    origin = (z == 0) & (k == 0)

    def pv_copies(m, view, src):
        d = 1 - 2 * (m % 2)
        along_z = remote(view(src, m), view(pv, m), pvz.at[m], pv_in.at[m], device(x, y, z + d + 4, k))
        across = remote(view(src, m), view(pv, m), pvc.at[m], pv_in.at[m], device(x, y, z, 1 - k))
        return along_z, (k == 0) & ((z * d + 8) % 4 < 3), across, k == 0

    def pv_case(m, act):
        @pl.when((m < 8) & origin)
        def _():
            act(pv_copies(m, rows, rp), True)

        @pl.when((m < 8) & ~origin)
        def _():
            act(pv_copies(m, rows, pv), False)

        @pl.when((m >= 8) & origin)
        def _():
            act(pv_copies(m, half, rp), True)

        @pl.when((m >= 8) & ~origin)
        def _():
            act(pv_copies(m, half, pv), False)

    def pv_event(m):
        def act(copies, first):
            az, pz, ac, pc = copies
            if not first:
                az.wait_recv()

            @pl.when(pz)
            def _():
                az.start()

            @pl.when(pc)
            def _():
                ac.start()

        pv_case(m, act)

    def xr_hop(m):
        d = 1 - 2 * (m % 2)
        c = rows(xr, m)
        along_z = remote(c, c, xrz.at[m], xr_in.at[m], device(x, y, z + d + 4, k))
        across = remote(c, c, xrc.at[m], xr_in.at[m], device(x, y, z, 1 - k))
        return along_z, (k == 0) & ((z * d + 8) % 4 < 3), across, k == 0

    def xr_event(m):
        az, pz, ac, pc = xr_hop(m)
        az.wait_recv()

        @pl.when(pz)
        def _():
            az.start()

        @pl.when(pc)
        def _():
            ac.start()

    def order(j):
        return 2 * (j // 4) + j % 2 + 8 * ((j % 4) // 2)

    def hook(h):
        j = h // 4

        @pl.when((h % 4 == 0) & (j < 16))
        def _():
            rp_event(order(j))

        @pl.when((h % 4 == 1) & (j >= 2) & (j < 18))
        def _():
            pv_event(order(j - 2))

        @pl.when((h % 4 == 2) & (j >= 10) & (j < 18))
        def _():
            xr_event(j - 10)

    @pl.when(me > 0)
    def _():
        to_before.wait_send()
        to_after.wait_recv()

    @pl.when(me < 127)
    def _():
        to_after.wait_send()
        to_before.wait_recv()

    applied[...] = jnp.zeros_like(applied)
    sub = lax.broadcasted_iota(jnp.int32, (256, 128), 0)

    def chunk(e, _):
        es = pl.ds(pl.multiple_of(e * 128, 128), 128)

        def gather(b, _):
            hook(e * 24 + b)
            got[b] = pick(ext, dofs[b, :, es], 18)
            return 0

        lax.fori_loop(0, 24, gather, 0)

        def contract(a4, _):
            total = [jnp.zeros((64, 128), F32) for _ in range(4)]
            for b in range(24):
                g = got[b]
                for q in range(4):
                    total[q] = total[q] + mass[a4 * 4 + q, pl.ds(b, 1), es] * g
            for q in range(4):
                a = a4 * 4 + q
                index = dofs[a, :, es]
                high = jnp.broadcast_to(index >> 8, (64, 128))
                low = jnp.broadcast_to(index & 255, (256, 128))
                big = total[q].astype(BF16).astype(F32)
                small = total[q] - big
                ps = pl.ds(pl.multiple_of(a * 128, 128), 128)
                for c in range(8):
                    here = high == c
                    wide[64 * c : 64 * c + 64, ps] = jnp.where(here, big, 0.0).astype(BF16)
                    wide[512 + 64 * c : 576 + 64 * c, ps] = jnp.where(here, small, 0.0).astype(BF16)
                hot[:, ps] = jnp.where(sub == low, 1.0, 0.0).astype(BF16)
            return 0

        lax.fori_loop(0, 6, contract, 0)
        out = lax.dot_general(wide[...], hot[...], NT, preferred_element_type=F32)
        for c in range(8):
            applied[:, 256 * c : 256 * c + 256] += out[64 * c : 64 * c + 64] + out[512 + 64 * c : 576 + 64 * c]
        return 0

    lax.fori_loop(0, 4, chunk, 0)

    def drain(m, _):
        ax, px, ay, py = rp_hop(m)

        @pl.when(px)
        def _():
            ax.wait_send()

        @pl.when(py)
        def _():
            ay.wait_send()

        def act(copies, first):
            az, pz, ac, pc = copies

            @pl.when(pz)
            def _():
                az.wait_send()

            @pl.when(pc)
            def _():
                ac.wait_send()

        pv_case(m, act)
        return 0

    lax.fori_loop(0, 16, drain, 0)

    def drain_x(m, _):
        az, pz, ac, pc = xr_hop(m)

        @pl.when(pz)
        def _():
            az.wait_send()

        @pl.when(pc)
        def _():
            ac.wait_send()
        return 0

    lax.fori_loop(0, 8, drain_x, 0)


def travel(front, vectors, dofs, faces, mass):
    dma = pltpu.SemaphoreType.DMA
    return pl.pallas_call(
        travel_kernel,
        out_shape=(
            jax.ShapeDtypeStruct((512, 1024), F32),
            jax.ShapeDtypeStruct((1024, 1024), F32),
            jax.ShapeDtypeStruct((1024, 1024), F32),
            jax.ShapeDtypeStruct((64, 2048), F32),
        ),
        in_specs=[VM] * 5,
        out_specs=(ANY, ANY, ANY, VM),
        scratch_shapes=[
            pltpu.VMEM((64, 2304), F32),
            pltpu.VMEM((2, 64, 128), F32),
            pltpu.VMEM((24, 64, 128), F32),
            pltpu.VMEM((1024, 3072), BF16),
            pltpu.VMEM((256, 3072), BF16),
            dma((16,)), dma((16,)), dma((8,)),
            dma((16,)), dma((16,)), dma((16,)), dma((16,)), dma((8,)), dma((8,)),
            dma((2,)), dma((2,)),
        ],
        compiler_params=pltpu.CompilerParams(collective_id=1, has_side_effects=True, vmem_limit_bytes=50 << 20),
    )(front, vectors, dofs, faces, mass)


def lanes(v, j):
    return jnp.broadcast_to(v[:, j : j + 1], (8, 128))


def subs(v, j):
    return jnp.broadcast_to(v[j : j + 1, :], (8, 128))


def tree(t):
    while len(t) > 1:
        t = [t[i] + t[i + 1] for i in range(0, len(t), 2)]
    return t[0]


def inverse8(cols, row8):
    cols = list(cols)
    for j in range(8):
        ip = 1.0 / subs(cols[j], j)
        pivot = cols[j]
        for m in range(8):
            if m != j:
                r = subs(cols[m], j) * ip
                cols[m] = jnp.where(row8 == j, r, cols[m] - pivot * r)
        cols[j] = jnp.where(row8 == j, ip, -pivot * ip)
    return cols


def inverse128(block):
    lane8 = lax.broadcasted_iota(jnp.int32, (8, 128), 1)
    row8 = lax.broadcasted_iota(jnp.int32, (8, 128), 0)
    v = [block[8 * i : 8 * i + 8] for i in range(16)]
    for kb in range(16):
        k0 = 8 * kb
        w = v[kb]
        cols = inverse8([lanes(w, k0 + j) for j in range(8)], row8)
        r = tree([cols[m] * subs(w, m) for m in range(8)])
        for m in range(8):
            r = jnp.where(lane8 == k0 + m, cols[m], r)
        rs = [subs(r, m) for m in range(8)]
        own = (lane8 // 8) == kb
        for i in list(range(kb + 1, 16)) + list(range(kb)):
            o = v[i]
            v[i] = jnp.where(own, 0.0, o) - tree([lanes(o, k0 + m) * rs[m] for m in range(8)])
        v[kb] = r
    return jnp.concatenate(v, 0)


def invert_in_place(ref):
    def body(b, _):
        s = pl.ds(pl.multiple_of(b * 128, 128), 128)
        d = inverse128(ref[s, s])
        c = ref[:, s]
        r = dot(d, ref[s, :])
        ref[...] = ref[...] - dot(c, r)
        ref[s, :] = r
        ref[:, s] = -dot(c, d)
        ref[s, s] = d
        return 0

    lax.fori_loop(0, 4, body, 0)


def update_kernel(bounds, diag, front, xr, rp, pv, out, a11, a12, a22, sem):
    row, col = lax.axis_index("row"), lax.axis_index("col")
    shift = (bounds[0] + bounds[1]).astype(F32) / 510.0

    def fetch(src):
        copies = [
            pltpu.make_async_copy(src.at[pl.ds(0, 512), pl.ds(0, 512)], a11, sem.at[0]),
            pltpu.make_async_copy(src.at[pl.ds(0, 512), pl.ds(512, 512)], a12, sem.at[1]),
            pltpu.make_async_copy(src.at[pl.ds(512, 512), pl.ds(512, 512)], a22, sem.at[2]),
        ]
        for c in copies:
            c.start()
        for c in copies:
            c.wait()

    @pl.when(col == 0)
    def _():
        fetch(rp)

    @pl.when(col > 0)
    def _():
        fetch(pv)

    ri = lax.broadcasted_iota(jnp.int32, (512, 512), 0)
    ci = lax.broadcasted_iota(jnp.int32, (512, 512), 1)
    a11[...] = a11[...] - jnp.where(ri == ci, shift * diag[:, 0:512], 0.0)
    a22[...] = a22[...] - jnp.where(ri == ci, shift * diag[:, 512:1024], 0.0)

    @pl.when((row == 0) & (col == 0))
    def _():
        out[:, 0:512] = a11[...]

    invert_in_place(a11)
    w = dot(a11[...], a12[...])
    s22 = a22[...] - dot(a12[...], w, TN)
    a12[...] = w
    a22[...] = s22

    @pl.when((row == 1) & (col == 0))
    def _():
        out[:, 0:512] = jnp.transpose(w)
        out[:, 512:1024] = s22

    @pl.when((row == 0) & (col == 0))
    def _():
        out[:, 512:1024] = w

    invert_in_place(a22)

    @pl.when(row >= 2)
    def _():
        x1, x2 = split(xr[:, 0:512]), xr[:, 512:1024]
        i2, ws = split(a22[...]), split(a12[...])
        l1 = dot3(x1, split(a11[...]))
        l2 = dot3(split(x2 - dot3(x1, ws)), i2)

        @pl.when(col == 0)
        def _():
            out[:, 0:512] = l1
            out[:, 512:1024] = l2

        @pl.when(col > 0)
        def _():
            l2s = split(l2)
            t1 = split(l1 - dot3(l2s, ws, NT))
            j = lax.broadcasted_iota(jnp.int32, (512, 1024), 1)
            i = lax.broadcasted_iota(jnp.int32, (512, 1024), 0)
            mine = diag[:, pl.ds(pl.multiple_of(col * 1024, 1024), 1024)]
            tile = front[...] - jnp.where(j + col * 1024 == i + row * 512, shift * mine, 0.0)
            out[...] = tile - dot3(t1, split(rp[0:512, :])) - dot3(l2s, split(rp[512:1024, :]))

    @pl.when((row == 0) & (col > 0))
    def _():
        out[...] = dot3(split(a11[...]), split(rp[0:512, :]))

    @pl.when((row == 1) & (col > 0))
    def _():
        out[...] = dot3(split(a22[...]), split(rp[512:1024, :] - dot3(split(a12[...]), split(rp[0:512, :]), TN)))


def update(bounds, diag, front, xr, rp, pv):
    return pl.pallas_call(
        update_kernel,
        out_shape=jax.ShapeDtypeStruct((512, 1024), F32),
        in_specs=[pl.BlockSpec(memory_space=pltpu.SMEM), VM, VM, VM, VM, ANY],
        out_specs=VM,
        scratch_shapes=[pltpu.VMEM((512, 512), F32)] * 3 + [pltpu.SemaphoreType.DMA((3,))],
        compiler_params=pltpu.CompilerParams(vmem_limit_bytes=56 << 20),
    )(bounds, diag, front, xr, rp, pv)


def lanczos_kernel(applied, basis, new, proj, chol, acc, slots, core_slot, send, recv):
    x, y, z, k = place()
    peers = [device(x + s, y, z, k) for s in (1, 2, 3)]
    peers += [device(x, y + s, z, k) for s in (1, 2, 3)]
    peers += [device(x, y, z + s, k) for s in (1, 2, 3)]
    peers += [device(x, y, z, 1 - k)]
    barrier = enter(peers)
    pl.semaphore_wait(barrier, len(peers))

    def reduce(phase, value):
        acc[phase, 0] = value
        c = remote(acc.at[phase, 0], core_slot.at[phase], send.at[phase, 9], recv.at[phase, 9], peers[9])
        c.start()
        c.wait()
        value = value + core_slot[phase]
        for axis, coordinate in enumerate((x, y, z)):
            acc[phase, axis + 1] = value
            copies = []
            for s in (1, 2, 3):
                n = 3 * axis + s - 1
                copies.append(
                    remote(
                        acc.at[phase, axis + 1], slots.at[phase, n], send.at[phase, n], recv.at[phase, n], peers[n]
                    )
                )
            for c in copies:
                c.start()
            for c in copies:
                c.wait()
            parts = [value] + [slots[phase, 3 * axis + s - 1] for s in (1, 2, 3)]
            ordered = []
            for q in range(4):
                away = (coordinate - q + 4) % 4
                part = parts[3]
                for s in (2, 1, 0):
                    part = jnp.where(away == s, parts[s], part)
                ordered.append(part)
            value = (ordered[0] + ordered[1]) + (ordered[2] + ordered[3])
        return value

    a = applied[...]
    pt = reduce(0, dot(a, basis[...], NT)) / TOTAL
    proj[...] = jnp.transpose(pt)
    corrected = a - dot(pt, basis[...])
    new[...] = corrected
    gram = dot(corrected, corrected, NT)
    gram = reduce(1, jnp.concatenate([gram, jnp.zeros((64, 64), F32)], axis=1)) / TOTAL

    lane8 = lax.broadcasted_iota(jnp.int32, (8, 128), 1)
    row8 = lax.broadcasted_iota(jnp.int32, (8, 128), 0)
    v = [gram[8 * i : 8 * i + 8] + jnp.where(lane8 == row8 + 64 + 8 * i, 1.0, 0.0) for i in range(8)]
    for kb in range(8):
        k0 = 8 * kb
        w = v[kb]
        first = [lanes(w, k0 + j) for j in range(8)]
        cols = inverse8(first, row8)
        r = tree([cols[m] * subs(w, m) for m in range(8)])
        rs = [subs(r, m) for m in range(8)]
        for i in range(kb + 1, 8):
            o = v[i]
            v[i] = o - tree([lanes(o, k0 + m) * rs[m] for m in range(8)])
        c = list(first)
        scale = jnp.zeros((8, 128), F32)
        for j in range(8):
            p = subs(c[j], j)
            f = jnp.where(row8 > j, c[j] / p, 0.0)
            w = w - f * subs(w, j)
            for m in range(j + 1, 8):
                c[m] = c[m] - f * subs(c[m], j)
            scale = jnp.where(row8 == j, p, scale)
        v[kb] = w / jnp.sqrt(scale)
    full = jnp.concatenate(v, 0)
    upper, inverse = full[:, 0:64], full[:, 64:128]
    ri = lax.broadcasted_iota(jnp.int32, (64, 64), 0)
    ci = lax.broadcasted_iota(jnp.int32, (64, 64), 1)
    chol[...] = jnp.transpose(jnp.where(ri <= ci, upper, 0.0))
    new[...] = dot(inverse, new[...])


def lanczos(applied, basis):
    dma = pltpu.SemaphoreType.DMA
    return pl.pallas_call(
        lanczos_kernel,
        out_shape=(
            jax.ShapeDtypeStruct((64, 2048), F32),
            jax.ShapeDtypeStruct((128, 64), F32),
            jax.ShapeDtypeStruct((64, 64), F32),
        ),
        in_specs=[VM, VM],
        out_specs=(VM, VM, VM),
        scratch_shapes=[
            pltpu.VMEM((2, 4, 64, 128), F32),
            pltpu.VMEM((2, 9, 64, 128), F32),
            pltpu.VMEM((2, 64, 128), F32),
            dma((2, 10)), dma((2, 10)),
        ],
        compiler_params=pltpu.CompilerParams(collective_id=2, has_side_effects=True, vmem_limit_bytes=40 << 20),
    )(applied, basis)


def shards(front, mass_diag, shift_bounds, vectors, basis, element_dofs, face_dofs, mass_blocks):
    xr, rp, pv, applied = travel(
        front, vectors, element_dofs.reshape(24, 1, 512), face_dofs.reshape(2, 1, 128), mass_blocks
    )
    new_block, projections, cholesky_factor = lanczos(applied, basis)
    factor = update(shift_bounds, mass_diag.reshape(1, -1), front, xr, rp, pv)
    return factor, new_block, projections, cholesky_factor


def solution(mesh):
    placed = (
        P("row", "col"),
        P(),
        P(),
        P(None, ("row", "col")),
        P(None, ("row", "col")),
        P(None, ("row", "col")),
        P(("row", "col"), None),
        P(None, None, ("row", "col")),
    )
    return jax.shard_map(
        shards,
        mesh=mesh,
        in_specs=placed,
        out_specs=(P("row", "col"), P(None, ("row", "col")), P(), P()),
        check_vma=False,
    )
```

time: 909 us -> 647 us (0.71); the launches traced: 895 us -> 643 us
  Pallas kernels: 0 us -> 636 us
  other arithmetic: 352 us -> 0 us
  waiting for transfers between devices: 205 us -> 0 us
  blocking collectives: 128 us -> 0 us
  local copies, waits for them, and re-layouts: 111 us -> 5.93 us
  matrix products: 72.6 us -> 0 us
  between operations: 21.1 us -> 0.69 us
    pallas_call x0 -> x3, Pallas kernels: none -> 636 us  [the longest x1 525 us: travel(): pl.pallas_call(travel_kernel, out_shape=(jax.ShapeDtypeStruct((512, 1024)...]
    another operation x41 -> x0, other arithmetic: 273 us -> none  [the longest x29 174 us: invert_block(): factor = jnp.linalg.cholesky(block)]
    psum x4 -> x0, waiting for transfers between devices: 204 us -> none  [from_root(): return lax.psum(kept, axis)]
    psum x2 -> x0, blocking collectives: 128 us -> none  [the longest x1 64.4 us: shards(): lax.psum(inner_rows(basis, applied), ('row', 'col')) / total_dofs]
    scatter-add x1 -> x0, other arithmetic: 66.4 us -> none  [shards(): jnp.zeros_like(extended).at[:, element_dofs].add(contrib)[:, :owned]]
    gather x3 -> x0, local copies, waits for them, and re-layouts: 45.9 us -> none  [the longest x1 41 us: shards(): gathered = extended[:, element_dofs]]
    dot_general x8 -> x0, matrix products: 41.9 us -> none  [the longest x5 21.9 us: product(): jnp.dot(left, right, precision=PRECISE, preferred_element_type=jnp.float32)]
    another operation x41 -> x0, matrix products: 30.7 us -> none  [the longest x28 16.1 us: invert_block(): return jax.scipy.linalg.cho_solve((factor, True), identity)]
  transfers between devices with their start and end apart: 6 -> 0, of which waited for: 3 -> 0; matrix products, arithmetic and copies ran while one was open for 39% -> 0% of each run, Pallas kernels for 0% -> 0%
where the time goes in v1:
time: 647 us; the launch traced here: 643 us
  Pallas kernels  636 us (98%)
    pallas_call x1, Pallas kernels, travel(): pl.pallas_call(travel_kernel, out_shape=(jax.ShapeDtypeStruct((512, 1024)...  525 us
    pallas_call x1, Pallas kernels, update(): pl.pallas_call(update_kernel, out_shape=jax.ShapeDtypeStruct((512, 1024),...  66.5 us
    pallas_call x1, Pallas kernels, lanczos(): pl.pallas_call(lanczos_kernel, out_shape=(jax.ShapeDtypeStruct((64, 2048)...  45.3 us

profile of v1, /device:TPU:42, one launch (start us, length us, event | category | flops | bytes accessed | tf_op | source)
XLA Modules:
  0.0 643.1 jit_solution(5754524167739239197)
XLA Ops:
  0.6 0.8 reshape.18.dofs
  1.5 0.0 copy-start
  1.5 1.3 copy-done
  2.7 0.0 copy-start.2
  2.7 1.0 copy-done.2
  3.8 0.0 copy-start.3
  3.8 0.7 copy-done.3
  4.5 524.7 %shard_map.111 = (f32[512,1024]{1,0:T(8,128)}, f32[1024,1024]{1,0:T(8,128)}, f32[1024,1024]{1,0:T(8,128)}, f32[64,2048]{1,0:T(8,128)S(1)}) custom-call(f32[512,1024]{1,0:T(8,128)} %front.3, f32[64,2048]{1,0:T(8,128)S(1)} %copy-done.2, s32[24,1,512]{2,1,0:T(1,128)S(1)} %reshape.18.dofs, s32[2,1,128]{2,1,0:T(1,128)S(1)} %bitcast.2, f32[24,24,512]{2,1,0:T(8,128)S(1)} %copy-done), custom_call_target="tpu_custom_call" | custom-call | tf_op jit(solution)/shard_map/pallas_call | solution.py:325
  529.2 0.0 copy-start.1
  529.2 66.5 %shard_map.112 = f32[512,1024]{1,0:T(8,128)} custom-call(s32[2]{0:T(128)} %bounds.1, f32[1,8192]{1,0:T(1,128)} %bitcast.3, f32[512,1024]{1,0:T(8,128)} %front.3, f32[512,1024]{1,0:T(8,128)} %get-tuple-element.11.xr, f32[1024,1024]{1,0:T(8,128)} %get-tuple-element.12.rp, f32[1024,1024]{1,0:T(8,128)} %get-tuple-element.13.pv), custom_call_target="tpu_custom_call" | custom-call | tf_op jit(solution)/shard_map/pallas_call | solution.py:492
  595.7 0.0 copy-done.1
  595.7 45.3 %shard_map.113 = (f32[64,2048]{1,0:T(8,128)S(1)}, f32[128,64]{1,0:T(8,128)S(1)}, f32[64,64]{1,0:T(8,128)S(1)}) custom-call(f32[64,2048]{1,0:T(8,128)S(1)} %get-tuple-element.14.applied, f32[128,2048]{1,0:T(8,128)S(1)} %copy-done.1), custom_call_target="tpu_custom_call" | custom-call | tf_op jit(solution)/shard_map/pallas_call | solution.py:583
  641.0 0.7 copy.12
  641.7 0.8 copy.15
  642.5 0.6 copy.16
Async XLA Ops:
  1.5 1.3 copy-start
  2.7 1.0 copy-start.2
  3.8 0.7 copy-start.3
  529.2 66.5 %copy-start.1 = (f32[128,2048]{1,0:T(8,128)S(1)}, f32[128,2048]{1,0:T(8,128)}, u32[]{:S(2)}) copy-start(f32[128,2048]{1,0:T(8,128)} %basis.1) | copy-start | bytes 3145732

commit v2 on v1

--- a/solution.py
+++ b/solution.py
@@ -11,7 +11,9 @@
 HI = lax.Precision.HIGHEST
 F32 = jnp.float32
 BF16 = jnp.bfloat16
-PB = 512
+STEP = 16
+LAG = 2
+NSTEP = 256 // STEP
 TOTAL = 262144.0
 VM = pl.BlockSpec(memory_space=pltpu.VMEM)
 ANY = pl.BlockSpec(memory_space=pl.ANY)
@@ -85,22 +87,31 @@
     ]
     barrier = enter(peers)
 
-    def rows(ref, m):
-        return ref.at[pl.ds(pl.multiple_of(m * 64, 64), 64), :]
-
-    def half(ref, m):
-        return ref.at[pl.ds(pl.multiple_of(m * 64, 64), 64), pl.ds(512, 512)]
+    def rows(ref, first, count=STEP):
+        return ref.at[pl.ds(pl.multiple_of(first, STEP), count), :]
+
+    def half(ref, first, count=STEP):
+        return ref.at[pl.ds(pl.multiple_of(first, STEP), count), pl.ds(512, 512)]
+
+    def ways():
+        return ((0, 1), (1, -1))
 
     for source in range(2):
         @pl.when((x == source) & (y == 0))
         def _():
-            for m in range(8):
-                pltpu.make_async_copy(rows(front, m), rows(rp, m + 8 * source), rp_in.at[m + 8 * source]).start()
+            for w, _ in ways():
+                for i in range(NSTEP):
+                    own = 256 * w + STEP * i
+                    pltpu.make_async_copy(
+                        rows(front, own), rows(rp, 512 * source + own), rp_in.at[2 * source + w, i]
+                    ).start()
 
     @pl.when((z == 0) & (k == 0))
     def _():
-        for m in range(8):
-            pltpu.make_async_copy(rows(front, m), rows(xr, m), xr_in.at[m]).start()
+        for w, _ in ways():
+            for i in range(NSTEP):
+                own = 256 * w + STEP * i
+                pltpu.make_async_copy(rows(front, own), rows(xr, own), xr_in.at[w, i]).start()
 
     ext[:, 0:2048] = vectors[...]
     fs[0] = pick(ext, faces[0], 16)
@@ -127,104 +138,86 @@
     def _():
         to_after.start()
 
-    def rp_hop(m):
-        d = 1 - 2 * (m % 2)
-        hx = ((x - m // 8) * d + 8) % 4
-        hy = (y * d + 8) % 4
-        c = rows(rp, m)
-        along_x = remote(c, c, rpx.at[m], rp_in.at[m], device(x + d + 4, y, z, k))
-        along_y = remote(c, c, rpy.at[m], rp_in.at[m], device(x, y + d + 4, z, k))
-        return along_x, (y == 0) & (hx < 3), along_y, hy < 3
-
-    def rp_event(m):
-        ax, px, ay, py = rp_hop(m)
-        ax.wait_recv()
-
-        @pl.when(px)
-        def _():
-            ax.start()
-
-        @pl.when(py)
-        def _():
-            ay.start()
-
     origin = (z == 0) & (k == 0)
 
-    def pv_copies(m, view, src):
-        d = 1 - 2 * (m % 2)
-        along_z = remote(view(src, m), view(pv, m), pvz.at[m], pv_in.at[m], device(x, y, z + d + 4, k))
-        across = remote(view(src, m), view(pv, m), pvc.at[m], pv_in.at[m], device(x, y, z, 1 - k))
-        return along_z, (k == 0) & ((z * d + 8) % 4 < 3), across, k == 0
-
-    def pv_case(m, act):
-        @pl.when((m < 8) & origin)
-        def _():
-            act(pv_copies(m, rows, rp), True)
-
-        @pl.when((m < 8) & ~origin)
-        def _():
-            act(pv_copies(m, rows, pv), False)
-
-        @pl.when((m >= 8) & origin)
-        def _():
-            act(pv_copies(m, half, rp), True)
-
-        @pl.when((m >= 8) & ~origin)
-        def _():
-            act(pv_copies(m, half, pv), False)
-
-    def pv_event(m):
-        def act(copies, first):
-            az, pz, ac, pc = copies
-            if not first:
-                az.wait_recv()
-
-            @pl.when(pz)
+    def rp_hop(source, w, d, i, count=STEP):
+        n = 2 * source + w
+        c = rows(rp, 512 * source + 256 * w + STEP * i, count)
+        hx, hy = ((x - source) * d + 8) % 4, (y * d + 8) % 4
+        return (
+            LAG * (hx + hy),
+            remote(c, c, rpx.at[n], rp_in.at[n, i], device(x + d + 4, y, z, k)), (y == 0) & (hx < 3),
+            remote(c, c, rpy.at[n], rp_in.at[n, i], device(x, y + d + 4, z, k)), hy < 3,
+        )
+
+    def pv_hop(source, w, d, i, src, count=STEP):
+        n = 2 * source + w
+        view = half if source else rows
+        first = 512 * source + 256 * w + STEP * i
+        hz = (z * d + 8) % 4
+        return (
+            LAG * (hz + k),
+            remote(view(src, first, count), view(pv, first, count), pvz.at[n], pv_in.at[n, i], device(x, y, z + d + 4, k)),
+            (k == 0) & (hz < 3),
+            remote(view(src, first, count), view(pv, first, count), pvc.at[n], pv_in.at[n, i], device(x, y, z, 1 - k)),
+            k == 0,
+        )
+
+    def xr_hop(w, d, i, count=STEP):
+        c = rows(xr, 256 * w + STEP * i, count)
+        hz = (z * d + 8) % 4
+        return (
+            LAG * (hz + k),
+            remote(c, c, xrz.at[w], xr_in.at[w, i], device(x, y, z + d + 4, k)), (k == 0) & (hz < 3),
+            remote(c, c, xrc.at[w], xr_in.at[w, i], device(x, y, z, 1 - k)), k == 0,
+        )
+
+    def pass_on(hop, received=True):
+        _, one, p1, two, p2 = hop
+        if received:
+            one.wait_recv()
+
+        @pl.when(p1)
+        def _():
+            one.start()
+
+        @pl.when(p2)
+        def _():
+            two.start()
+
+    def slot(t):
+        for w, d in ways():
+            i = t - xr_hop(w, d, 0)[0]
+
+            @pl.when((i >= 0) & (i < NSTEP))
             def _():
-                az.start()
-
-            @pl.when(pc)
-            def _():
-                ac.start()
-
-        pv_case(m, act)
-
-    def xr_hop(m):
-        d = 1 - 2 * (m % 2)
-        c = rows(xr, m)
-        along_z = remote(c, c, xrz.at[m], xr_in.at[m], device(x, y, z + d + 4, k))
-        across = remote(c, c, xrc.at[m], xr_in.at[m], device(x, y, z, 1 - k))
-        return along_z, (k == 0) & ((z * d + 8) % 4 < 3), across, k == 0
-
-    def xr_event(m):
-        az, pz, ac, pc = xr_hop(m)
-        az.wait_recv()
-
-        @pl.when(pz)
-        def _():
-            az.start()
-
-        @pl.when(pc)
-        def _():
-            ac.start()
-
-    def order(j):
-        return 2 * (j // 4) + j % 2 + 8 * ((j % 4) // 2)
+                pass_on(xr_hop(w, d, i))
+
+        for source in range(2):
+            for w, d in ways():
+                i = t - rp_hop(source, w, d, 0)[0]
+
+                @pl.when((i >= 0) & (i < NSTEP))
+                def _():
+                    pass_on(rp_hop(source, w, d, i))
+
+        for source in range(2):
+            for w, d in ways():
+                i = t - rp_hop(source, w, d, 0)[0] - pv_hop(source, w, d, 0, pv)[0]
+                due = (i >= 0) & (i < NSTEP)
+
+                @pl.when(due & origin)
+                def _():
+                    pass_on(pv_hop(source, w, d, i, rp), False)
+
+                @pl.when(due & ~origin)
+                def _():
+                    pass_on(pv_hop(source, w, d, i, pv))
 
     def hook(h):
-        j = h // 4
-
-        @pl.when((h % 4 == 0) & (j < 16))
-        def _():
-            rp_event(order(j))
-
-        @pl.when((h % 4 == 1) & (j >= 2) & (j < 18))
-        def _():
-            pv_event(order(j - 2))
-
-        @pl.when((h % 4 == 2) & (j >= 10) & (j < 18))
-        def _():
-            xr_event(j - 10)
+        @pl.when((h % 2 == 0) & (h < 2 * (NSTEP + 10 * LAG)))
+        def _():
+            slot(h // 2)
 
     @pl.when(me > 0)
     def _():
@@ -278,46 +271,22 @@
 
     lax.fori_loop(0, 4, chunk, 0)
 
-    def drain(m, _):
-        ax, px, ay, py = rp_hop(m)
-
-        @pl.when(px)
-        def _():
-            ax.wait_send()
-
-        @pl.when(py)
-        def _():
-            ay.wait_send()
-
-        def act(copies, first):
-            az, pz, ac, pc = copies
-
-            @pl.when(pz)
-            def _():
-                az.wait_send()
-
-            @pl.when(pc)
-            def _():
-                ac.wait_send()
-
-        pv_case(m, act)
-        return 0
-
-    lax.fori_loop(0, 16, drain, 0)
-
-    def drain_x(m, _):
-        az, pz, ac, pc = xr_hop(m)
-
-        @pl.when(pz)
-        def _():
-            az.wait_send()
-
-        @pl.when(pc)
-        def _():
-            ac.wait_send()
-        return 0
-
-    lax.fori_loop(0, 8, drain_x, 0)
+    def drain(hop):
+        _, one, p1, two, p2 = hop
+
+        @pl.when(p1)
+        def _():
+            one.wait_send()
+
+        @pl.when(p2)
+        def _():
+            two.wait_send()
+
+    for w, d in ways():
+        drain(xr_hop(w, d, 0, 256))
+        for source in range(2):
+            drain(rp_hop(source, w, d, 0, 256))
+            drain(pv_hop(source, w, d, 0, pv, 256))
 
 
 def travel(front, vectors, dofs, faces, mass):
@@ -338,8 +307,8 @@
             pltpu.VMEM((24, 64, 128), F32),
             pltpu.VMEM((1024, 3072), BF16),
             pltpu.VMEM((256, 3072), BF16),
-            dma((16,)), dma((16,)), dma((8,)),
-            dma((16,)), dma((16,)), dma((16,)), dma((16,)), dma((8,)), dma((8,)),
+            dma((4, NSTEP)), dma((4, NSTEP)), dma((2, NSTEP)),
+            dma((4,)), dma((4,)), dma((4,)), dma((4,)), dma((2,)), dma((2,)),
             dma((2,)), dma((2,)),
         ],
         compiler_params=pltpu.CompilerParams(collective_id=1, has_side_effects=True, vmem_limit_bytes=50 << 20),

time: 647 us -> 226 us (0.35)
  Pallas kernels: 636 us -> 215 us
    pallas_call x1, Pallas kernels: 525 us -> 114 us  [travel(): pl.pallas_call(travel_kernel, out_shape=(jax.ShapeDtypeStruct((512, 1024)...]
    pallas_call x1, Pallas kernels: 45.3 us -> 35.4 us  [lanczos(): pl.pallas_call(lanczos_kernel, out_shape=(jax.ShapeDtypeStruct((64, 2048)...]
where the time goes in v2:
time: 226 us; the launch traced here: 222 us
  Pallas kernels  215 us (95%)
  local copies, waits for them, and re-layouts  5.93 us (3%)
    pallas_call x1, Pallas kernels, travel(): pl.pallas_call(travel_kernel, out_shape=(jax.ShapeDtypeStruct((512, 1024)...  114 us
    pallas_call x1, Pallas kernels, update(): pl.pallas_call(update_kernel, out_shape=jax.ShapeDtypeStruct((512, 1024),...  66.5 us
    pallas_call x1, Pallas kernels, lanczos(): pl.pallas_call(lanczos_kernel, out_shape=(jax.ShapeDtypeStruct((64, 2048)...  35.4 us
    unnamed x11, local copies, waits for them, and re-layouts  5.1 us

profile of v2, /device:TPU:42, one launch (start us, length us, event | category | flops | bytes accessed | tf_op | source)
XLA Modules:
  0.0 222.1 jit_solution(13318053538759207326)
XLA Ops:
  0.6 0.8 reshape.18.dofs
  1.5 0.0 copy-start
  1.5 1.3 copy-done
  2.7 0.0 copy-start.2
  2.7 1.0 copy-done.2
  3.8 0.0 copy-start.3
  3.8 0.7 copy-done.3
  4.5 113.6 %shard_map.111 = (f32[512,1024]{1,0:T(8,128)}, f32[1024,1024]{1,0:T(8,128)}, f32[1024,1024]{1,0:T(8,128)}, f32[64,2048]{1,0:T(8,128)S(1)}) custom-call(f32[512,1024]{1,0:T(8,128)} %front.3, f32[64,2048]{1,0:T(8,128)S(1)} %copy-done.2, s32[24,1,512]{2,1,0:T(1,128)S(1)} %reshape.18.dofs, s32[2,1,128]{2,1,0:T(1,128)S(1)} %bitcast.2, f32[24,24,512]{2,1,0:T(8,128)S(1)} %copy-done), custom_call_target="tpu_custom_call" | custom-call | tf_op jit(solution)/shard_map/pallas_call | solution.py:294
  118.1 0.0 copy-start.1
  118.1 66.5 %shard_map.112 = f32[512,1024]{1,0:T(8,128)} custom-call(s32[2]{0:T(128)} %bounds.1, f32[1,8192]{1,0:T(1,128)} %bitcast.3, f32[512,1024]{1,0:T(8,128)} %front.3, f32[512,1024]{1,0:T(8,128)} %get-tuple-element.11.xr, f32[1024,1024]{1,0:T(8,128)} %get-tuple-element.12.rp, f32[1024,1024]{1,0:T(8,128)} %get-tuple-element.13.pv), custom_call_target="tpu_custom_call" | custom-call | tf_op jit(solution)/shard_map/pallas_call | solution.py:461
  184.6 0.0 copy-done.1
  184.6 35.4 %shard_map.113 = (f32[64,2048]{1,0:T(8,128)S(1)}, f32[128,64]{1,0:T(8,128)S(1)}, f32[64,64]{1,0:T(8,128)S(1)}) custom-call(f32[64,2048]{1,0:T(8,128)S(1)} %get-tuple-element.14.applied, f32[128,2048]{1,0:T(8,128)S(1)} %copy-done.1), custom_call_target="tpu_custom_call" | custom-call | tf_op jit(solution)/shard_map/pallas_call | solution.py:552
  220.0 0.7 copy.12
  220.7 0.8 copy.15
  221.5 0.6 copy.16
Async XLA Ops:
  1.5 1.3 copy-start
  2.7 1.0 copy-start.2
  3.8 0.7 copy-start.3
  118.1 66.5 %copy-start.1 = (f32[128,2048]{1,0:T(8,128)S(1)}, f32[128,2048]{1,0:T(8,128)}, u32[]{:S(2)}) copy-start(f32[128,2048]{1,0:T(8,128)} %basis.1) | copy-start | bytes 3145732

commit v3 on v2

v3 whole, which is shorter than its diff:
```python
import functools

import jax
import jax.numpy as jnp
from jax import lax
from jax.experimental import pallas as pl
from jax.experimental.pallas import tpu as pltpu
from jax.sharding import PartitionSpec as P

MESH = pl.DeviceIdType.MESH
HI = lax.Precision.HIGHEST
F32 = jnp.float32
BF16 = jnp.bfloat16
STEP = 32
LAG = 2
NSTEP = 256 // STEP
TOTAL = 262144.0
VM = pl.BlockSpec(memory_space=pltpu.VMEM)
ANY = pl.BlockSpec(memory_space=pl.ANY)
NT = (((1,), (1,)), ((), ()))
NN = (((1,), (0,)), ((), ()))
TN = (((0,), (0,)), ((), ()))


def dot(a, b, dims=NN):
    return lax.dot_general(a, b, dims, precision=HI, preferred_element_type=F32)


def split(a):
    high = a.astype(BF16)
    return high, (a - high.astype(F32)).astype(BF16)


def dot3(a, b, dims=NN):
    (ah, al), (bh, bl) = a, b

    def one(l, r):
        return lax.dot_general(l, r, dims, preferred_element_type=F32)

    return one(ah, bh) + (one(ah, bl) + one(al, bh))


def place():
    row, col = lax.axis_index("row"), lax.axis_index("col")
    return row % 4, row // 4, col // 2, col % 2


def device(x, y, z, k):
    return ((y % 4) * 4 + (x % 4), (z % 4) * 2 + k)


def enter(peers):
    barrier = pltpu.get_barrier_semaphore()
    for peer in peers:
        pl.semaphore_signal(barrier, inc=1, device_id=peer, device_id_type=MESH)
    return barrier


def remote(src, dst, send, recv, peer):
    return pltpu.make_async_remote_copy(
        src_ref=src, dst_ref=dst, send_sem=send, recv_sem=recv, device_id=peer, device_id_type=MESH
    )


def lanes(v, j):
    return jnp.broadcast_to(v[:, j : j + 1], (8, 128))


def subs(v, j):
    return jnp.broadcast_to(v[j : j + 1, :], (8, 128))


def tree(t):
    while len(t) > 1:
        t = [t[i] + t[i + 1] for i in range(0, len(t), 2)]
    return t[0]


def inverse8(cols, row8):
    cols = list(cols)
    for j in range(8):
        ip = 1.0 / subs(cols[j], j)
        pivot = cols[j]
        for m in range(8):
            if m != j:
                r = subs(cols[m], j) * ip
                cols[m] = jnp.where(row8 == j, r, cols[m] - pivot * r)
        cols[j] = jnp.where(row8 == j, ip, -pivot * ip)
    return cols


def inverse128(block, between):
    lane8 = lax.broadcasted_iota(jnp.int32, (8, 128), 1)
    row8 = lax.broadcasted_iota(jnp.int32, (8, 128), 0)
    v = [block[8 * i : 8 * i + 8] for i in range(16)]
    for kb in range(16):
        if kb % 4 == 0:
            between(kb // 4)
        k0 = 8 * kb
        w = v[kb]
        cols = inverse8([lanes(w, k0 + j) for j in range(8)], row8)
        r = tree([cols[m] * subs(w, m) for m in range(8)])
        for m in range(8):
            r = jnp.where(lane8 == k0 + m, cols[m], r)
        rs = [subs(r, m) for m in range(8)]
        own = (lane8 // 8) == kb
        for i in list(range(kb + 1, 16)) + list(range(kb)):
            o = v[i]
            v[i] = jnp.where(own, 0.0, o) - tree([lanes(o, k0 + m) * rs[m] for m in range(8)])
        v[kb] = r
    return jnp.concatenate(v, 0)


def invert_in_place(ref, between, after):
    def body(b, _):
        s = pl.ds(pl.multiple_of(b * 128, 128), 128)
        d = inverse128(ref[s, s], functools.partial(between, b))
        c = ref[:, s]
        r = dot(d, ref[s, :])
        ref[...] = ref[...] - dot(c, r)
        ref[s, :] = r
        ref[:, s] = -dot(c, d)
        ref[s, s] = d
        after(b)
        return 0

    lax.fori_loop(0, 4, body, 0)


def pick(ext_ref, index, chunks):
    low = jnp.broadcast_to(index & 127, (64, 128))
    high = jnp.broadcast_to(index >> 7, (64, 128))
    found = jnp.take_along_axis(ext_ref[:, 0:128], low, axis=1)
    for c in range(1, chunks):
        found = jnp.where(high == c, jnp.take_along_axis(ext_ref[:, 128 * c : 128 * c + 128], low, axis=1), found)
    return found


def step_kernel(
    bounds, diag, vectors, dofs, faces, front, mass_hbm, basis_hbm,
    out, new, proj, chol,
    xr, rp, pv, applied, ext, fs, got, wide, hot, mass, basis, a11, a12, a22, acc, slots, core_slot,
    rp_in, pv_in, xr_in, rpx, rpy, pvz, pvc, xrz, xrc, face_out, face_in, load, send, recv,
):
    x, y, z, k = place()
    me = lax.axis_index("row") * 8 + lax.axis_index("col")
    before, after = (me + 127) % 128, (me + 1) % 128
    peers = [
        device(x + 1, y, z, k), device(x + 3, y, z, k), device(x, y + 1, z, k), device(x, y + 3, z, k),
        device(x, y, z + 1, k), device(x, y, z + 3, k), device(x, y, z, 1 - k),
        (before // 8, before % 8), (after // 8, after % 8),
        device(x + 2, y, z, k), device(x, y + 2, z, k), device(x, y, z + 2, k),
    ]
    barrier = enter(peers)
    on_x = [[lax.rem((x - source) * d + 8, 4) for d in (1, -1)] for source in range(2)]
    on_y = [lax.rem(y * d + 8, 4) for d in (1, -1)]
    on_z = [lax.rem(z * d + 8, 4) for d in (1, -1)]
    next_x, next_y, next_z = peers[0:2], peers[2:4], peers[4:6]
    other = peers[6]
    far_x = [[(y == 0) & (on_x[source][w] < 3) for w in range(2)] for source in range(2)]
    far_y = [on_y[w] < 3 for w in range(2)]
    far_z = [(k == 0) & (on_z[w] < 3) for w in range(2)]
    first_core = k == 0
    lag_xy = [[LAG * (on_x[source][w] + on_y[w]) for w in range(2)] for source in range(2)]
    lag_z = [LAG * (on_z[w] + k) for w in range(2)]

    def rows(ref, first, count=STEP):
        return ref.at[pl.ds(pl.multiple_of(first, STEP), count), :]

    def half(ref, first, count=STEP):
        return ref.at[pl.ds(pl.multiple_of(first, STEP), count), pl.ds(512, 512)]

    def ways():
        return ((0, 1), (1, -1))

    loads = [
        pltpu.make_async_copy(mass_hbm, mass, load.at[0]),
        pltpu.make_async_copy(basis_hbm, basis, load.at[1]),
        pltpu.make_async_copy(front, out, load.at[2]),
    ]
    for c in loads:
        c.start()

    origin = (z == 0) & (k == 0)

    def own_piece(source, view):
        for w, _ in ways():
            for i in range(NSTEP):
                own = 256 * w + STEP * i
                pltpu.make_async_copy(
                    view(front, own), view(rp, 512 * source + own), rp_in.at[2 * source + w, i]
                ).start()

    @pl.when((x == 0) & (y == 0))
    def _():
        own_piece(0, rows)

    @pl.when((x == 1) & (y == 0) & origin)
    def _():
        own_piece(1, half)

    @pl.when((x == 1) & (y == 0) & ~origin)
    def _():
        own_piece(1, rows)

    @pl.when((z == 0) & (k == 0))
    def _():
        for w, _ in ways():
            for i in range(NSTEP):
                own = 256 * w + STEP * i
                pltpu.make_async_copy(rows(front, own), rows(xr, own), xr_in.at[w, i]).start()

    ext[:, 0:2048] = vectors[...]
    fs[0] = pick(ext, faces[0], 16)
    fs[1] = pick(ext, faces[1], 16)

    @pl.when(me == 0)
    def _():
        ext[:, 2048:2176] = jnp.zeros((64, 128), F32)

    @pl.when(me == 127)
    def _():
        ext[:, 2176:2304] = jnp.zeros((64, 128), F32)

    pl.semaphore_wait(barrier, len(peers))

    to_before = remote(fs.at[0], ext.at[:, pl.ds(2176, 128)], face_out.at[0], face_in.at[0], (before // 8, before % 8))
    to_after = remote(fs.at[1], ext.at[:, pl.ds(2048, 128)], face_out.at[1], face_in.at[1], (after // 8, after % 8))

    @pl.when(me > 0)
    def _():
        to_before.start()

    @pl.when(me < 127)
    def _():
        to_after.start()

    def rp_hop(source, w, d, i, count=STEP, view=rows):
        n = 2 * source + w
        c = view(rp, 512 * source + 256 * w + STEP * i, count)
        return (
            remote(c, c, rpx.at[n], rp_in.at[n, i], next_x[w]), far_x[source][w],
            remote(c, c, rpy.at[n], rp_in.at[n, i], next_y[w]), far_y[w],
        )

    def pv_hop(source, w, d, i, src, count=STEP):
        n = 2 * source + w
        view = half if source else rows
        first = 512 * source + 256 * w + STEP * i
        return (
            remote(view(src, first, count), view(pv, first, count), pvz.at[n], pv_in.at[n, i], next_z[w]), far_z[w],
            remote(view(src, first, count), view(pv, first, count), pvc.at[n], pv_in.at[n, i], other), first_core,
        )

    def xr_hop(w, d, i, count=STEP):
        c = rows(xr, 256 * w + STEP * i, count)
        return (
            remote(c, c, xrz.at[w], xr_in.at[w, i], next_z[w]), far_z[w],
            remote(c, c, xrc.at[w], xr_in.at[w, i], other), first_core,
        )

    def pass_on(hop, received=True):
        one, p1, two, p2 = hop
        if received:
            one.wait_recv()

        @pl.when(p1)
        def _():
            one.start()

        @pl.when(p2)
        def _():
            two.start()

    def pivot_slot(t):
        for source in range(2):
            view = half if source else rows
            for w, d in ways():
                i = t - NSTEP * source - lag_xy[source][w]

                @pl.when(origin & (i >= 0) & (i < NSTEP))
                def _():
                    pass_on(rp_hop(source, w, d, i, STEP, view))
                    pass_on(pv_hop(source, w, d, i, rp), False)

                j = i - lag_z[w]

                @pl.when(~origin & (j >= 0) & (j < NSTEP))
                def _():
                    pass_on(pv_hop(source, w, d, j, pv))

    def panel_slot(t):
        for source in range(2):
            for w, d in ways():
                i = t - NSTEP * source - lag_xy[source][w]

                @pl.when(~origin & (i >= 0) & (i < NSTEP))
                def _():
                    pass_on(rp_hop(source, w, d, i))

        for w, d in ways():
            i = t - 12 - lag_z[w]

            @pl.when((i >= 0) & (i < NSTEP))
            def _():
                pass_on(xr_hop(w, d, i))

    def gather_hook(e, b):
        @pl.when(lax.rem(b, 6) == 0)
        def _():
            pivot_slot(7 * e + lax.div(b, 6))

        @pl.when(lax.rem(b, 12) == 3)
        def _():
            panel_slot(3 * e + lax.div(b, 12))

    def contract_hook(e, a4):
        @pl.when(lax.rem(a4, 2) == 0)
        def _():
            pivot_slot(7 * e + 4 + lax.div(a4, 2))

        @pl.when(a4 == 3)
        def _():
            panel_slot(3 * e + 2)

    @pl.when(me > 0)
    def _():
        to_before.wait_send()
        to_after.wait_recv()

    @pl.when(me < 127)
    def _():
        to_after.wait_send()
        to_before.wait_recv()

    applied[...] = jnp.zeros_like(applied)
    loads[0].wait()
    sub = lax.broadcasted_iota(jnp.int32, (256, 128), 0)

    def chunk(e, _):
        es = pl.ds(pl.multiple_of(e * 128, 128), 128)

        def gather(b, _):
            gather_hook(e, b)
            got[b] = pick(ext, dofs[b, :, es], 18)
            return 0

        lax.fori_loop(0, 24, gather, 0)

        def contract(a4, _):
            contract_hook(e, a4)
            total = [jnp.zeros((64, 128), F32) for _ in range(4)]
            for b in range(24):
                g = got[b]
                for q in range(4):
                    total[q] = total[q] + mass[a4 * 4 + q, pl.ds(b, 1), es] * g
            for q in range(4):
                a = a4 * 4 + q
                index = dofs[a, :, es]
                high = jnp.broadcast_to(index >> 8, (64, 128))
                low = jnp.broadcast_to(index & 255, (256, 128))
                big = total[q].astype(BF16).astype(F32)
                small = total[q] - big
                ps = pl.ds(pl.multiple_of(a * 128, 128), 128)
                for c in range(8):
                    here = high == c
                    wide[64 * c : 64 * c + 64, ps] = jnp.where(here, big, 0.0).astype(BF16)
                    wide[512 + 64 * c : 576 + 64 * c, ps] = jnp.where(here, small, 0.0).astype(BF16)
                hot[:, ps] = jnp.where(sub == low, 1.0, 0.0).astype(BF16)
            return 0

        lax.fori_loop(0, 6, contract, 0)
        out = lax.dot_general(wide[...], hot[...], NT, preferred_element_type=F32)
        for c in range(8):
            applied[:, 256 * c : 256 * c + 256] += out[64 * c : 64 * c + 64] + out[512 + 64 * c : 576 + 64 * c]
        return 0

    lax.fori_loop(0, 4, chunk, 0)

    lines = [device(x, y, z, 1 - k)]
    lines += [device(x + s, y, z, k) for s in (1, 2, 3)]
    lines += [device(x, y + s, z, k) for s in (1, 2, 3)]
    lines += [device(x, y, z + s, k) for s in (1, 2, 3)]

    def sum_copies(phase, stage):
        if stage == 0:
            return [remote(acc.at[phase, 0], core_slot.at[phase], send.at[phase, 0], recv.at[phase, 0], lines[0])]
        return [
            remote(acc.at[phase, stage], slots.at[phase, n - 1], send.at[phase, n], recv.at[phase, n], lines[n])
            for n in range(3 * stage - 2, 3 * stage + 1)
        ]

    def start_sum(phase, stage):
        for c in sum_copies(phase, stage):
            c.start()

    def finish_sum(phase, stage):
        for c in sum_copies(phase, stage):
            c.wait()
        value = acc[phase, stage]
        if stage == 0:
            acc[phase, 1] = value + core_slot[phase]
            return
        coordinate = (x, y, z)[stage - 1]
        parts = [value] + [slots[phase, 3 * stage - 4 + s] for s in (1, 2, 3)]
        ordered = []
        for q in range(4):
            away = (coordinate - q + 4) % 4
            part = parts[3]
            for s in (2, 1, 0):
                part = jnp.where(away == s, parts[s], part)
            ordered.append(part)
        acc[phase, stage + 1] = (ordered[0] + ordered[1]) + (ordered[2] + ordered[3])

    row, col = lax.axis_index("row"), lax.axis_index("col")
    shift = (bounds[0] + bounds[1]).astype(F32) / 510.0
    ri = lax.broadcasted_iota(jnp.int32, (512, 512), 0)
    ci = lax.broadcasted_iota(jnp.int32, (512, 512), 1)

    def pivot(ref, r, c, shifted):
        for where, src in ((col == 0, rp), (col > 0, pv)):
            @pl.when(where)
            def _():
                block = src[r : r + 512, c : c + 512]
                if shifted:
                    block = block - jnp.where(ri == ci, shift * diag[:, c : c + 512], 0.0)
                ref[...] = block

    loads[1].wait()
    acc[0, 0] = dot(applied[...], basis[...], NT)
    start_sum(0, 0)
    loads[2].wait()
    pivot(a11, 0, 0, True)

    @pl.when((row == 0) & (col == 0))
    def _():
        out[:, 0:512] = a11[...]

    def first_slots(b, q):
        if q % 2 == 0:
            pivot_slot(28 + 2 * b + q // 2)
        else:
            panel_slot(12 + 2 * b + q // 2)

    def last_slots(b, q):
        if q % 2 == 1:
            panel_slot(20 + 2 * b + q // 2)

    def advance(phase, b):
        for stage in range(4):
            @pl.when(b == stage)
            def _():
                finish_sum(phase, stage)
                if stage < 3:
                    start_sum(phase, stage + 1)

    invert_in_place(a11, first_slots, functools.partial(advance, 0))

    pt = acc[0, 4] / TOTAL
    proj[...] = jnp.transpose(pt)
    corrected = applied[...] - dot(pt, basis[...])
    applied[...] = corrected
    acc[1, 0] = jnp.concatenate([dot(corrected, corrected, NT), jnp.zeros((64, 64), F32)], axis=1)
    start_sum(1, 0)

    pivot(a12, 0, 512, False)
    pivot(a22, 512, 512, True)
    w = dot(a11[...], a12[...])
    s22 = a22[...] - dot(a12[...], w, TN)
    a12[...] = w
    a22[...] = s22

    @pl.when((row == 1) & (col == 0))
    def _():
        out[:, 0:512] = jnp.transpose(w)
        out[:, 512:1024] = s22

    @pl.when((row == 0) & (col == 0))
    def _():
        out[:, 512:1024] = w

    invert_in_place(a22, last_slots, functools.partial(advance, 1))

    @pl.when(row >= 2)
    def _():
        x1, x2 = split(xr[:, 0:512]), xr[:, 512:1024]
        i2, ws = split(a22[...]), split(a12[...])
        l1 = dot3(x1, split(a11[...]))
        l2 = dot3(split(x2 - dot3(x1, ws)), i2)

        @pl.when(col == 0)
        def _():
            out[:, 0:512] = l1
            out[:, 512:1024] = l2

        @pl.when(col > 0)
        def _():
            l2s = split(l2)
            t1 = split(l1 - dot3(l2s, ws, NT))
            j = lax.broadcasted_iota(jnp.int32, (512, 1024), 1)
            i = lax.broadcasted_iota(jnp.int32, (512, 1024), 0)
            mine = diag[:, pl.ds(pl.multiple_of(col * 1024, 1024), 1024)]
            tile = out[...] - jnp.where(j + col * 1024 == i + row * 512, shift * mine, 0.0)
            out[...] = tile - dot3(t1, split(rp[0:512, :])) - dot3(l2s, split(rp[512:1024, :]))

    @pl.when((row == 0) & (col > 0))
    def _():
        out[...] = dot3(split(a11[...]), split(rp[0:512, :]))

    @pl.when((row == 1) & (col > 0))
    def _():
        out[...] = dot3(split(a22[...]), split(rp[512:1024, :] - dot3(split(a12[...]), split(rp[0:512, :]), TN)))

    gram = acc[1, 4] / TOTAL
    lane8 = lax.broadcasted_iota(jnp.int32, (8, 128), 1)
    row8 = lax.broadcasted_iota(jnp.int32, (8, 128), 0)
    v = [gram[8 * i : 8 * i + 8] + jnp.where(lane8 == row8 + 64 + 8 * i, 1.0, 0.0) for i in range(8)]
    for kb in range(8):
        k0 = 8 * kb
        w = v[kb]
        first = [lanes(w, k0 + j) for j in range(8)]
        cols = inverse8(first, row8)
        r = tree([cols[m] * subs(w, m) for m in range(8)])
        rs = [subs(r, m) for m in range(8)]
        for i in range(kb + 1, 8):
            o = v[i]
            v[i] = o - tree([lanes(o, k0 + m) * rs[m] for m in range(8)])
        c = list(first)
        scale = jnp.zeros((8, 128), F32)
        for j in range(8):
            p = subs(c[j], j)
            f = jnp.where(row8 > j, c[j] / p, 0.0)
            w = w - f * subs(w, j)
            for m in range(j + 1, 8):
                c[m] = c[m] - f * subs(c[m], j)
            scale = jnp.where(row8 == j, p, scale)
        v[kb] = w / jnp.sqrt(scale)
    full = jnp.concatenate(v, 0)
    upper, inverse = full[:, 0:64], full[:, 64:128]
    ri = lax.broadcasted_iota(jnp.int32, (64, 64), 0)
    ci = lax.broadcasted_iota(jnp.int32, (64, 64), 1)
    chol[...] = jnp.transpose(jnp.where(ri <= ci, upper, 0.0))
    new[...] = dot(inverse, applied[...])

    def drain(hop):
        one, p1, two, p2 = hop

        @pl.when(p1)
        def _():
            one.wait_send()

        @pl.when(p2)
        def _():
            two.wait_send()

    for w, d in ways():
        drain(xr_hop(w, d, 0, 256))
        drain(rp_hop(0, w, d, 0, 256))

        @pl.when(origin)
        def _():
            drain(rp_hop(1, w, d, 0, 256, half))

        @pl.when(~origin)
        def _():
            drain(rp_hop(1, w, d, 0, 256))

        for source in range(2):
            drain(pv_hop(source, w, d, 0, pv, 256))


def step(bounds, diag, vectors, dofs, faces, front, mass, basis):
    dma = pltpu.SemaphoreType.DMA
    return pl.pallas_call(
        step_kernel,
        out_shape=(
            jax.ShapeDtypeStruct((512, 1024), F32),
            jax.ShapeDtypeStruct((64, 2048), F32),
            jax.ShapeDtypeStruct((128, 64), F32),
            jax.ShapeDtypeStruct((64, 64), F32),
        ),
        in_specs=[pl.BlockSpec(memory_space=pltpu.SMEM), VM, VM, VM, VM, ANY, ANY, ANY],
        out_specs=(VM, VM, VM, VM),
        scratch_shapes=[
            pltpu.VMEM((512, 1024), F32),
            pltpu.VMEM((1024, 1024), F32),
            pltpu.VMEM((1024, 1024), F32),
            pltpu.VMEM((64, 2048), F32),
            pltpu.VMEM((64, 2304), F32),
            pltpu.VMEM((2, 64, 128), F32),
            pltpu.VMEM((24, 64, 128), F32),
            pltpu.VMEM((1024, 3072), BF16),
            pltpu.VMEM((256, 3072), BF16),
            pltpu.VMEM((24, 24, 512), F32),
            pltpu.VMEM((128, 2048), F32),
            pltpu.VMEM((512, 512), F32),
            pltpu.VMEM((512, 512), F32),
            pltpu.VMEM((512, 512), F32),
            pltpu.VMEM((2, 5, 64, 128), F32),
            pltpu.VMEM((2, 9, 64, 128), F32),
            pltpu.VMEM((2, 64, 128), F32),
            dma((4, NSTEP)), dma((4, NSTEP)), dma((2, NSTEP)),
            dma((4,)), dma((4,)), dma((4,)), dma((4,)), dma((2,)), dma((2,)),
            dma((2,)), dma((2,)), dma((3,)), dma((2, 10)), dma((2, 10)),
        ],
        compiler_params=pltpu.CompilerParams(collective_id=1, has_side_effects=True, vmem_limit_bytes=60 << 20),
    )(bounds, diag, vectors, dofs, faces, front, mass, basis)


def shards(front, mass_diag, shift_bounds, vectors, basis, element_dofs, face_dofs, mass_blocks):
    return step(
        shift_bounds, mass_diag.reshape(1, -1), vectors,
        element_dofs.reshape(24, 1, 512), face_dofs.reshape(2, 1, 128), front, mass_blocks, basis,
    )


def solution(mesh):
    placed = (
        P("row", "col"),
        P(),
        P(),
        P(None, ("row", "col")),
        P(None, ("row", "col")),
        P(None, ("row", "col")),
        P(("row", "col"), None),
        P(None, None, ("row", "col")),
    )
    return jax.shard_map(
        shards,
        mesh=mesh,
        in_specs=placed,
        out_specs=(P("row", "col"), P(None, ("row", "col")), P(), P()),
        check_vma=False,
    )
```

time: 226 us -> 169 us (0.75); the launches traced: 222 us -> 169 us
  Pallas kernels: 215 us -> 160 us
    pallas_call x3 -> x1, Pallas kernels: 215 us -> 160 us  [step(): pl.pallas_call(step_kernel, out_shape=(jax.ShapeDtypeStruct((512, 1024),...]
    unnamed x11 -> x7, local copies, waits for them, and re-layouts: 5.1 us -> 4.63 us
where the time goes in v3:
time: 169 us
  Pallas kernels  160 us (95%)
  local copies, waits for them, and re-layouts  7.62 us (5%)
    pallas_call x1, Pallas kernels, step(): pl.pallas_call(step_kernel, out_shape=(jax.ShapeDtypeStruct((512, 1024),...  160 us
    unnamed x7, local copies, waits for them, and re-layouts  4.63 us

profile of v3, /device:TPU:42, one launch (start us, length us, event | category | flops | bytes accessed | tf_op | source)
XLA Modules:
  0.0 168.6 jit_solution(1424333532314374894)
XLA Ops:
  0.6 1.5 reshape.18.dofs
  2.1 160.4 %shard_map.111 = (f32[512,1024]{1,0:T(8,128)}, f32[64,2048]{1,0:T(8,128)}, f32[128,64]{1,0:T(8,128)}, f32[64,64]{1,0:T(8,128)}) custom-call(s32[2]{0:T(128)} %bounds.1, f32[1,8192]{1,0:T(1,128)} %bitcast.2, f32[64,2048]{1,0:T(8,128)} %vectors.1, s32[24,1,512]{2,1,0:T(1,128)} %reshape.18.dofs, s32[2,1,128]{2,1,0:T(1,128)} %bitcast.3, f32[512,1024]{1,0:T(8,128)} %front.1, ...), custom_call_target="tpu_custom_call" | custom-call | tf_op jit(solution)/shard_map/pallas_call | solution.py:574
  162.5 1.5 copy.12
  164.0 0.0 copy-start
  164.0 0.0 copy-start.1
  164.0 3.2 %copy.16 = f32[512,1024]{1,0:T(8,128)} copy(f32[512,1024]{1,0:T(8,128)} %get-tuple-element.12) | data formatting | bytes 4194304
  167.2 0.0 copy-done
  167.2 0.8 copy.17
  168.0 0.0 copy-done.1
  168.0 0.6 copy.18
Async XLA Ops:
  164.0 3.2 %copy-start = (f32[64,2048]{1,0:T(8,128)S(1)}, f32[64,2048]{1,0:T(8,128)}, u32[]{:S(2)}) copy-start(f32[64,2048]{1,0:T(8,128)} %get-tuple-element.13) | copy-start | bytes 1572868
  164.0 4.0 %copy-start.1 = (f32[64,64]{1,0:T(8,128)S(1)}, f32[64,64]{1,0:T(8,128)}, u32[]{:S(2)}) copy-start(f32[64,64]{1,0:T(8,128)} %get-tuple-element.15) | copy-start | bytes 49156

commit v4 on v3

--- a/solution.py
+++ b/solution.py
@@ -137,10 +137,10 @@
 
 
 def step_kernel(
-    bounds, diag, vectors, dofs, faces, front, mass_hbm, basis_hbm,
+    bounds, diag, vectors, dofs_in, faces, front, mass_hbm, basis_hbm,
     out, new, proj, chol,
-    xr, rp, pv, applied, ext, fs, got, wide, hot, mass, basis, a11, a12, a22, acc, slots, core_slot,
-    rp_in, pv_in, xr_in, rpx, rpy, pvz, pvc, xrz, xrc, face_out, face_in, load, send, recv,
+    dofs, xr, rp, pv, applied, ext, fs, got, wide, hot, mass, basis, a11, a12, a22, acc, slots, core_slot,
+    rp_in, pn_in, pnx, pny, pv_in, xr_in, rpx, rpy, pvz, pvc, xrz, xrc, face_out, face_in, load, send, recv,
 ):
     x, y, z, k = place()
     me = lax.axis_index("row") * 8 + lax.axis_index("col")
@@ -162,13 +162,19 @@
     far_z = [(k == 0) & (on_z[w] < 3) for w in range(2)]
     first_core = k == 0
     lag_xy = [[LAG * (on_x[source][w] + on_y[w]) for w in range(2)] for source in range(2)]
+    late = [(y == 0) & (x != source) for source in range(2)]
+    lag_yx = [[LAG * (on_x[source][w] + on_y[w] + jnp.where(late[source], 4, 0)) for w in range(2)] for source in range(2)]
+    b_far_x = [[(y != 0) & (on_x[source][w] < 3) for w in range(2)] for source in range(2)]
+    b_far_y = [
+        [((x == source) & (on_y[w] < 3)) | ((x != source) & (on_y[w] == 3)) for w in range(2)] for source in range(2)
+    ]
     lag_z = [LAG * (on_z[w] + k) for w in range(2)]
 
     def rows(ref, first, count=STEP):
-        return ref.at[pl.ds(pl.multiple_of(first, STEP), count), :]
+        return ref.at[pl.ds(pl.multiple_of(first, 16), count), :]
 
     def half(ref, first, count=STEP):
-        return ref.at[pl.ds(pl.multiple_of(first, STEP), count), pl.ds(512, 512)]
+        return ref.at[pl.ds(pl.multiple_of(first, 16), count), pl.ds(512, 512)]
 
     def ways():
         return ((0, 1), (1, -1))
@@ -191,7 +197,15 @@
                     view(front, own), view(rp, 512 * source + own), rp_in.at[2 * source + w, i]
                 ).start()
 
-    @pl.when((x == 0) & (y == 0))
+    def own_panel(source):
+        for w, _ in ways():
+            for i in range(16):
+                own = 256 * w + 16 * i
+                pltpu.make_async_copy(
+                    rows(front, own, 16), rows(rp, 512 * source + own, 16), pn_in.at[2 * source + w, i]
+                ).start()
+
+    @pl.when((x == 0) & (y == 0) & origin)
     def _():
         own_piece(0, rows)
 
@@ -199,9 +213,13 @@
     def _():
         own_piece(1, half)
 
+    @pl.when((x == 0) & (y == 0) & ~origin)
+    def _():
+        own_panel(0)
+
     @pl.when((x == 1) & (y == 0) & ~origin)
     def _():
-        own_piece(1, rows)
+        own_panel(1)
 
     @pl.when((z == 0) & (k == 0))
     def _():
@@ -211,8 +229,10 @@
                 pltpu.make_async_copy(rows(front, own), rows(xr, own), xr_in.at[w, i]).start()
 
     ext[:, 0:2048] = vectors[...]
-    fs[0] = pick(ext, faces[0], 16)
-    fs[1] = pick(ext, faces[1], 16)
+    fs[0] = pick(ext, faces[0:1, :], 16)
+    fs[1] = pick(ext, faces[1:2, :], 16)
+    for b in range(24):
+        dofs[b] = dofs_in[b : b + 1, :]
 
     @pl.when(me == 0)
     def _():
@@ -241,6 +261,16 @@
         return (
             remote(c, c, rpx.at[n], rp_in.at[n, i], next_x[w]), far_x[source][w],
             remote(c, c, rpy.at[n], rp_in.at[n, i], next_y[w]), far_y[w],
+        )
+
+    def panel_hop(source, w, kind, i, count=16):
+        n = 2 * source + w
+        c = rows(rp, 512 * source + 256 * w + 128 * kind + 16 * i, count)
+        return (
+            remote(c, c, pnx.at[n + 4 * kind], pn_in.at[n, i + 8 * kind], next_x[w]),
+            b_far_x[source][w] if kind else far_x[source][w],
+            remote(c, c, pny.at[n + 4 * kind], pn_in.at[n, i + 8 * kind], next_y[w]),
+            b_far_y[source][w] if kind else far_y[w],
         )
 
     def pv_hop(source, w, d, i, src, count=STEP):
@@ -291,15 +321,16 @@
 
     def panel_slot(t):
         for source in range(2):
-            for w, d in ways():
-                i = t - NSTEP * source - lag_xy[source][w]
-
-                @pl.when(~origin & (i >= 0) & (i < NSTEP))
-                def _():
-                    pass_on(rp_hop(source, w, d, i))
+            for w, _ in ways():
+                for kind, lag in ((0, lag_xy[source][w]), (1, lag_yx[source][w])):
+                    i = t - 8 * source - lag
+
+                    @pl.when(~origin & (i >= 0) & (i < 8))
+                    def _():
+                        pass_on(panel_hop(source, w, kind, i))
 
         for w, d in ways():
-            i = t - 12 - lag_z[w]
+            i = t - 14 - lag_z[w]
 
             @pl.when((i >= 0) & (i < NSTEP))
             def _():
@@ -312,16 +343,16 @@
 
         @pl.when(lax.rem(b, 12) == 3)
         def _():
-            panel_slot(3 * e + lax.div(b, 12))
+            panel_slot(4 * e + lax.div(b, 12))
 
     def contract_hook(e, a4):
         @pl.when(lax.rem(a4, 2) == 0)
         def _():
             pivot_slot(7 * e + 4 + lax.div(a4, 2))
 
-        @pl.when(a4 == 3)
-        def _():
-            panel_slot(3 * e + 2)
+        @pl.when((a4 == 1) | (a4 == 3))
+        def _():
+            panel_slot(4 * e + 2 + lax.div(a4, 2))
 
     @pl.when(me > 0)
     def _():
@@ -440,11 +471,11 @@
         if q % 2 == 0:
             pivot_slot(28 + 2 * b + q // 2)
         else:
-            panel_slot(12 + 2 * b + q // 2)
+            panel_slot(16 + 2 * b + q // 2)
 
     def last_slots(b, q):
         if q % 2 == 1:
-            panel_slot(20 + 2 * b + q // 2)
+            panel_slot(24 + 2 * b + q // 2)
 
     def advance(phase, b):
         for stage in range(4):
@@ -457,7 +488,7 @@
     invert_in_place(a11, first_slots, functools.partial(advance, 0))
 
     pt = acc[0, 4] / TOTAL
-    proj[...] = jnp.transpose(pt)
+    proj[...] = pt
     corrected = applied[...] - dot(pt, basis[...])
     applied[...] = corrected
     acc[1, 0] = jnp.concatenate([dot(corrected, corrected, NT), jnp.zeros((64, 64), F32)], axis=1)
@@ -555,15 +586,17 @@
 
     for w, d in ways():
         drain(xr_hop(w, d, 0, 256))
-        drain(rp_hop(0, w, d, 0, 256))
 
         @pl.when(origin)
         def _():
+            drain(rp_hop(0, w, d, 0, 256))
             drain(rp_hop(1, w, d, 0, 256, half))
 
         @pl.when(~origin)
         def _():
-            drain(rp_hop(1, w, d, 0, 256))
+            for source in range(2):
+                for kind in range(2):
+                    drain(panel_hop(source, w, kind, 0, 128))
 
         for source in range(2):
             drain(pv_hop(source, w, d, 0, pv, 256))
@@ -576,12 +609,13 @@
         out_shape=(
             jax.ShapeDtypeStruct((512, 1024), F32),
             jax.ShapeDtypeStruct((64, 2048), F32),
-            jax.ShapeDtypeStruct((128, 64), F32),
+            jax.ShapeDtypeStruct((64, 128), F32),
             jax.ShapeDtypeStruct((64, 64), F32),
         ),
         in_specs=[pl.BlockSpec(memory_space=pltpu.SMEM), VM, VM, VM, VM, ANY, ANY, ANY],
         out_specs=(VM, VM, VM, VM),
         scratch_shapes=[
+            pltpu.VMEM((24, 1, 512), jnp.int32),
             pltpu.VMEM((512, 1024), F32),
             pltpu.VMEM((1024, 1024), F32),
             pltpu.VMEM((1024, 1024), F32),
@@ -599,7 +633,7 @@
             pltpu.VMEM((2, 5, 64, 128), F32),
             pltpu.VMEM((2, 9, 64, 128), F32),
             pltpu.VMEM((2, 64, 128), F32),
-            dma((4, NSTEP)), dma((4, NSTEP)), dma((2, NSTEP)),
+            dma((4, NSTEP)), dma((4, 16)), dma((8,)), dma((8,)), dma((4, NSTEP)), dma((2, NSTEP)),
             dma((4,)), dma((4,)), dma((4,)), dma((4,)), dma((2,)), dma((2,)),
             dma((2,)), dma((2,)), dma((3,)), dma((2, 10)), dma((2, 10)),
         ],
@@ -608,10 +642,11 @@
 
 
 def shards(front, mass_diag, shift_bounds, vectors, basis, element_dofs, face_dofs, mass_blocks):
-    return step(
+    factor, new_block, projections, cholesky_factor = step(
         shift_bounds, mass_diag.reshape(1, -1), vectors,
-        element_dofs.reshape(24, 1, 512), face_dofs.reshape(2, 1, 128), front, mass_blocks, basis,
+        element_dofs, face_dofs, front, mass_blocks, basis,
     )
+    return factor, new_block, projections.T, cholesky_factor
 
 
 def solution(mesh):

time: 169 us -> 155 us (0.917)
  Pallas kernels: 160 us -> 149 us
  local copies, waits for them, and re-layouts: 7.62 us -> 5.25 us
    pallas_call x1, Pallas kernels: 160 us -> 149 us  [step(): pl.pallas_call(step_kernel, out_shape=(jax.ShapeDtypeStruct((512, 1024),...]
    unnamed x7 -> x10, local copies, waits for them, and re-layouts: 4.63 us -> 5.25 us
where the time goes in v4:
time: 155 us
  Pallas kernels  149 us (96%)
  local copies, waits for them, and re-layouts  5.25 us (3%)
    pallas_call x1, Pallas kernels, step(): pl.pallas_call(step_kernel, out_shape=(jax.ShapeDtypeStruct((512, 1024),...  149 us
    unnamed x10, local copies, waits for them, and re-layouts  5.25 us

profile of v4, /device:TPU:42, one launch (start us, length us, event | category | flops | bytes accessed | tf_op | source)
XLA Modules:
  0.0 154.8 jit_solution(14151377597136050559)
XLA Ops:
  0.6 148.9 %shard_map.111 = (f32[512,1024]{1,0:T(8,128)}, f32[64,2048]{1,0:T(8,128)}, f32[64,128]{1,0:T(8,128)}, f32[64,64]{1,0:T(8,128)}) custom-call(s32[2]{0:T(128)} %bounds.1, f32[1,8192]{1,0:T(1,128)} %bitcast.2, f32[64,2048]{1,0:T(8,128)} %vectors.1, s32[24,512]{1,0:T(8,128)} %dofs_in.1, s32[2,128]{1,0:T(2,128)} %faces.1, f32[512,1024]{1,0:T(8,128)} %front.1, ...), custom_call_target="tpu_custom_call" | custom-call | tf_op jit(solution)/shard_map/pallas_call | solution.py:607
  149.5 0.0 copy-start
  149.5 0.0 copy-start.2
  149.5 0.0 copy-start.1
  149.5 3.2 %copy.16 = f32[512,1024]{1,0:T(8,128)} copy(f32[512,1024]{1,0:T(8,128)} %get-tuple-element.16) | data formatting | bytes 4194304
  152.8 0.0 copy-done
  152.8 0.8 copy.17
  153.5 0.0 copy-done.2
  153.6 0.6 copy.18
  154.2 0.0 copy-done.1
  154.2 0.6 copy.19
Async XLA Ops:
  149.5 3.2 %copy-start = (f32[64,2048]{1,0:T(8,128)S(1)}, f32[64,2048]{1,0:T(8,128)}, u32[]{:S(2)}) copy-start(f32[64,2048]{1,0:T(8,128)} %get-tuple-element.17) | copy-start | bytes 1572868
  149.5 4.0 %copy-start.2 = (f32[64,128]{1,0:T(8,128)S(1)}, f32[64,128]{1,0:T(8,128)}, u32[]{:S(2)}) copy-start(f32[64,128]{1,0:T(8,128)} %get-tuple-element.10) | copy-start | bytes 98308
  149.5 4.6 %copy-start.1 = (f32[64,64]{1,0:T(8,128)S(1)}, f32[64,64]{1,0:T(8,128)}, u32[]{:S(2)}) copy-start(f32[64,64]{1,0:T(8,128)} %get-tuple-element.19) | copy-start | bytes 49156

commit v5 on v4

--- a/solution.py
+++ b/solution.py
@@ -164,6 +164,12 @@
     lag_xy = [[LAG * (on_x[source][w] + on_y[w]) for w in range(2)] for source in range(2)]
     late = [(y == 0) & (x != source) for source in range(2)]
     lag_yx = [[LAG * (on_x[source][w] + on_y[w] + jnp.where(late[source], 4, 0)) for w in range(2)] for source in range(2)]
+    side = [(y != 0) & (x == source) for source in range(2)]
+    lag_a = [[LAG * (on_x[source][w] + on_y[w] + jnp.where(side[source], 4, 0)) for w in range(2)] for source in range(2)]
+    a_far_x = [
+        [((y == 0) & (on_x[source][w] < 3)) | ((y != 0) & (on_x[source][w] == 3)) for w in range(2)] for source in range(2)
+    ]
+    a_far_y = [[(x != source) & (on_y[w] < 3) for w in range(2)] for source in range(2)]
     b_far_x = [[(y != 0) & (on_x[source][w] < 3) for w in range(2)] for source in range(2)]
     b_far_y = [
         [((x == source) & (on_y[w] < 3)) | ((x != source) & (on_y[w] == 3)) for w in range(2)] for source in range(2)
@@ -268,9 +274,9 @@
         c = rows(rp, 512 * source + 256 * w + 128 * kind + 16 * i, count)
         return (
             remote(c, c, pnx.at[n + 4 * kind], pn_in.at[n, i + 8 * kind], next_x[w]),
-            b_far_x[source][w] if kind else far_x[source][w],
+            b_far_x[source][w] if kind else a_far_x[source][w],
             remote(c, c, pny.at[n + 4 * kind], pn_in.at[n, i + 8 * kind], next_y[w]),
-            b_far_y[source][w] if kind else far_y[w],
+            b_far_y[source][w] if kind else a_far_y[source][w],
         )
 
     def pv_hop(source, w, d, i, src, count=STEP):
@@ -322,7 +328,7 @@
     def panel_slot(t):
         for source in range(2):
             for w, _ in ways():
-                for kind, lag in ((0, lag_xy[source][w]), (1, lag_yx[source][w])):
+                for kind, lag in ((0, lag_a[source][w]), (1, lag_yx[source][w])):
                     i = t - 8 * source - lag
 
                     @pl.when(~origin & (i >= 0) & (i < 8))

time: 155 us -> 153 us (0.987)
  Pallas kernels: 149 us -> 147 us
    pallas_call x1, Pallas kernels: 149 us -> 147 us  [step(): pl.pallas_call(step_kernel, out_shape=(jax.ShapeDtypeStruct((512, 1024),...]
where the time goes in v5:
time: 153 us; the launch traced here: 152 us
  Pallas kernels  147 us (96%)
  local copies, waits for them, and re-layouts  5.25 us (3%)
    pallas_call x1, Pallas kernels, step(): pl.pallas_call(step_kernel, out_shape=(jax.ShapeDtypeStruct((512, 1024),...  147 us
    unnamed x10, local copies, waits for them, and re-layouts  5.25 us

profile of v5, /device:TPU:42, one launch (start us, length us, event | category | flops | bytes accessed | tf_op | source)
XLA Modules:
  0.0 152.5 jit_solution(16298614919652893550)
XLA Ops:
  0.6 146.6 %shard_map.111 = (f32[512,1024]{1,0:T(8,128)}, f32[64,2048]{1,0:T(8,128)}, f32[64,128]{1,0:T(8,128)}, f32[64,64]{1,0:T(8,128)}) custom-call(s32[2]{0:T(128)} %bounds.1, f32[1,8192]{1,0:T(1,128)} %bitcast.2, f32[64,2048]{1,0:T(8,128)} %vectors.1, s32[24,512]{1,0:T(8,128)} %dofs_in.1, s32[2,128]{1,0:T(2,128)} %faces.1, f32[512,1024]{1,0:T(8,128)} %front.1, ...), custom_call_target="tpu_custom_call" | custom-call | tf_op jit(solution)/shard_map/pallas_call | solution.py:613
  147.2 0.0 copy-start
  147.2 0.0 copy-start.2
  147.2 0.0 copy-start.1
  147.2 3.2 %copy.16 = f32[512,1024]{1,0:T(8,128)} copy(f32[512,1024]{1,0:T(8,128)} %get-tuple-element.16) | data formatting | bytes 4194304
  150.5 0.0 copy-done
  150.5 0.8 copy.17
  151.3 0.0 copy-done.2
  151.3 0.6 copy.18
  151.9 0.0 copy-done.1
  151.9 0.6 copy.19
Async XLA Ops:
  147.2 3.2 %copy-start = (f32[64,2048]{1,0:T(8,128)S(1)}, f32[64,2048]{1,0:T(8,128)}, u32[]{:S(2)}) copy-start(f32[64,2048]{1,0:T(8,128)} %get-tuple-element.17) | copy-start | bytes 1572868
  147.2 4.0 %copy-start.2 = (f32[64,128]{1,0:T(8,128)S(1)}, f32[64,128]{1,0:T(8,128)}, u32[]{:S(2)}) copy-start(f32[64,128]{1,0:T(8,128)} %get-tuple-element.10) | copy-start | bytes 98308
  147.2 4.6 %copy-start.1 = (f32[64,64]{1,0:T(8,128)S(1)}, f32[64,64]{1,0:T(8,128)}, u32[]{:S(2)}) copy-start(f32[64,64]{1,0:T(8,128)} %get-tuple-element.19) | copy-start | bytes 49156
